TPU v7x, 128 devices: a whole 4x4x4 slice. The times are simulated.
128 devices in a mesh: rows: 16 (over y, x), cols: 8 (over z, core).
Axes of the slice: x: 4, y: 4, z: 4, core: 2. Of those that a mesh axis runs over, the one named last changes fastest.
Arguments:
- latent: bfloat16 [512, 512, 320], P('rows', 'cols'), may hold values from -100 to 100
- conv_weights: bfloat16 [5, 2880, 320], P(None, 'rows'), may hold values from -0.109375 to 0.109375
- conv_bias: float32 [5, 320], replicated, may hold values from -4 to 4
- norm_gain: float32 [4, 320], replicated, may hold values from 0.25 to 1.75
- norm_shift: float32 [4, 320], replicated, may hold values from -4 to 4
- time_shift: float32 [2, 320], replicated, may hold values from -5 to 5
Outputs:
- features: bfloat16 [512, 512, 320], P('rows', 'cols')
- reduced: bfloat16 [256, 256, 320], P('rows', 'cols')
All inputs are finite; a program needn't handle non-finite values.
Results may differ from a plain program's by a relative error of at most 0.01.
Values may be sent and summed in bfloat16 or wider, within the bound.
A program may use at most 128 MiB of HBM per device.

v0:
```python
import functools

import jax
import jax.numpy as jnp
from jax import lax
from jax.sharding import Mesh
from jax.sharding import PartitionSpec as P

GROUPS = 32
ROWS = ("rows_0", "rows_1")
COLS = ("cols_0", "cols_1")
ROWS_COLS = ("rows_0", "rows_1", "cols_0", "cols_1")


eps = 1e-05


def by_axis(value, axes):
    return functools.reduce(lax.psum, axes, value)


def extended(cells, sides, width):
    for axis, dim in sides:
        count = lax.axis_size(axis)
        ends = count - 1
        head = lax.slice_in_dim(cells, 0, width, axis=dim)
        tail = lax.slice_in_dim(cells, cells.shape[dim] - width, cells.shape[dim], axis=dim)
        cells = jnp.concatenate(
            [
                lax.ppermute(tail, axis, [(i, (i + 1) % count) for i in range(ends)]),
                cells,
                lax.ppermute(head, axis, [((i + 1) % count, i) for i in range(ends)]),
            ],
            axis=dim,
        )
    return cells


def from_everyone(value, axis):
    copies = jnp.broadcast_to(value, (lax.axis_size(axis), *value.shape))
    return lax.all_to_all(copies, axis, split_axis=0, concat_axis=0, tiled=True)


def laid_out(tiles, dim):
    lengths = list(tiles.shape[1:])
    lengths[dim] *= tiles.shape[0]
    return jnp.moveaxis(tiles, 0, dim).reshape(lengths)


def collect(value, axis, dim):
    tiles = from_everyone(value, axis)
    return laid_out(tiles, dim)


def to_groups(per_channel):
    return jnp.sum(per_channel.reshape(GROUPS, -1), axis=1)


def to_channels(per_group, width):
    return jnp.repeat(per_group, width // GROUPS)


def group_norm(act, gain, shift):
    width = act.shape[2]
    values = act.astype(jnp.float32)
    total_count = (
        act.shape[0] * lax.axis_size(ROWS) * act.shape[1] * lax.axis_size(COLS) * (width // GROUPS)
    )
    sums, squares = (
        by_axis(to_groups(jnp.sum(values, axis=(0, 1))), ROWS_COLS),
        by_axis(to_groups(jnp.sum(values * values, axis=(0, 1))), ROWS_COLS),
    )
    mean = sums / total_count
    spread = squares / total_count - mean * mean
    mean_chan = to_channels(mean, width)
    deviate = values - mean_chan
    scale_chan = to_channels(lax.rsqrt(spread + eps), width) * gain
    scaled = deviate * scale_chan + shift
    return jax.nn.silu(scaled).astype(jnp.bfloat16)


def conv_local(padded, kernel_rows, stride):
    width_in = padded.shape[2]
    kernel = kernel_rows.reshape(3, 3, width_in, kernel_rows.shape[1])
    result = lax.conv_general_dilated(
        padded[None],
        kernel,
        (stride, stride),
        "VALID",
        dimension_numbers=("NHWC", "HWIO", "NHWC"),
        preferred_element_type=jnp.float32,
    )
    return result[0]


def convolve(act, weight_local, bias, stride):
    padded = extended(act, ((ROWS, 0), (COLS, 1)), 1)
    width = act.shape[2]
    empty = jnp.zeros((9 * width, width), jnp.bfloat16)
    kernel = lax.dynamic_update_slice_in_dim(empty, collect(weight_local, ROWS, 0), jnp.int32(0), 0)
    result = conv_local(padded, kernel, stride)
    return result + bias


def local(latent, conv_weights, conv_bias, norm_gain, norm_shift, time_shift):
    current = latent
    for block in range(2):
        first = 2 * block
        normed = group_norm(current, norm_gain[first], norm_shift[first])
        inner = (
            convolve(normed, conv_weights[first], conv_bias[first], 1) + time_shift[block]
        ).astype(jnp.bfloat16)
        normed = group_norm(inner, norm_gain[first + 1], norm_shift[first + 1])
        branch = convolve(normed, conv_weights[first + 1], conv_bias[first + 1], 1)
        current = (current.astype(jnp.float32) + branch).astype(jnp.bfloat16)
    reduced = convolve(current, conv_weights[4], conv_bias[4], 2).astype(jnp.bfloat16)
    return (current, reduced)


def solution(mesh):
    split = Mesh(mesh.devices.reshape(4, 4, 4, 2), ("rows_0", "rows_1", "cols_0", "cols_1"))
    placed = (P(ROWS, COLS, None), P(None, ROWS, None), P(), P(), P(), P())
    return jax.shard_map(
        local,
        mesh=split,
        in_specs=placed,
        out_specs=(P(ROWS, COLS, None), P(ROWS, COLS, None)),
        check_vma=False,
    )
```

profile of v0, /device:TPU:1, one launch (start us, length us, event | category | flops | bytes accessed | tf_op | source)
XLA Modules:
  0.0 379.9 jit_solution(18384742968063074915)
XLA Ops:
  4.2 7.8 %all-to-all-start = ((bf16[16,180,320]{2,1,0:T(8,128)(2,1)}), bf16[16,180,320]{2,1,0:T(8,128)(2,1)}, u32[]{:S(2)}, u32[]{:S(2)}) async-start(bf16[16,180,320]{2,1,0:T(8,128)(2,1)} %broadcast_in_dim.61), calls=%async_computation | async-start | bytes 4521984 | tf_op jit(solution)/shard_map/all_to_all | solution.py:41
  13.4 20.3 %all-reduce.11 = (f32[32]{0:T(128)S(1)}, f32[32]{0:T(128)S(1)}) all-reduce(f32[32]{0:T(128)S(1)} %reduce_sum.147, f32[32]{0:T(128)S(1)} %reduce_sum.145), channel_id=1, replica_groups=mesh['rows_0'=4,'rows_1'=4,'cols_0'=4,'cols_1'=2] {'rows_0'}, use_global_device_ids=true, to_apply=%region_8.0 | all-reduce | flops 64 | bytes 512 | tf_op jit(solution)/shard_map/psum | solution.py:19
  33.7 15.8 %all-reduce.7 = (f32[32]{0:T(128)S(1)}, f32[32]{0:T(128)S(1)}) all-reduce(f32[32]{0:T(128)S(1)} %get-tuple-element.49, f32[32]{0:T(128)S(1)} %get-tuple-element.50), channel_id=1, replica_groups=mesh['rows_0'=4,'rows_1'=4,'cols_0'=4,'cols_1'=2] {'rows_1'}, use_global_device_ids=true, to_apply=%region_9.0 | all-reduce | flops 64 | bytes 512 | tf_op jit(solution)/shard_map/psum | solution.py:19
  49.5 9.7 %all-reduce.3 = (f32[32]{0:T(128)S(1)}, f32[32]{0:T(128)S(1)}) all-reduce(f32[32]{0:T(128)S(1)} %get-tuple-element.41, f32[32]{0:T(128)S(1)} %get-tuple-element.42), channel_id=1, replica_groups=mesh['rows_0'=4,'rows_1'=4,'cols_0'=4,'cols_1'=2] {'cols_0'}, use_global_device_ids=true, to_apply=%region_10.0 | all-reduce | flops 64 | bytes 512 | tf_op jit(solution)/shard_map/psum | solution.py:19
  59.3 8.6 %all-reduce.15 = (f32[32]{0:T(128)S(1)}, f32[32]{0:T(128)S(1)}) all-reduce(f32[32]{0:T(128)S(1)} %get-tuple-element.33, f32[32]{0:T(128)S(1)} %get-tuple-element.34), channel_id=1, replica_groups=mesh['rows_0'=4,'rows_1'=4,'cols_0'=4,'cols_1'=2] {'cols_1'}, use_global_device_ids=true, to_apply=%region_11.0 | all-reduce | flops 64 | bytes 512 | tf_op jit(solution)/shard_map/psum | solution.py:19
  74.5 3.8 collective-permute-done.1
  80.3 2.5 collective-permute-start.3
  83.4 2.1 collective-permute-done.3
  88.0 2.5 broadcast_in_dim.65
  90.5 7.1 %all-to-all-start.1 = ((bf16[16,180,320]{2,1,0:T(8,128)(2,1)}), bf16[16,180,320]{2,1,0:T(8,128)(2,1)}, u32[]{:S(2)}, u32[]{:S(2)}) async-start(bf16[16,180,320]{2,1,0:T(8,128)(2,1)} %broadcast_in_dim.65), calls=%async_computation.1 | async-start | bytes 4521984 | tf_op jit(solution)/shard_map/all_to_all | solution.py:41
  97.6 4.2 %reshape_reshape.15 = bf16[3,3,320,320]{3,2,1,0:T(8,128)(2,1)} reshape(bf16[16,180,320]{2,1,0:T(8,128)(2,1)} %all-to-all-done) | data formatting | bytes 3686400 | tf_op jit(solution)/shard_map/reshape;reshape | solution.py:84
  101.9 9.7 %fusion.95 = f32[32,8,9,320]{3,1,2,0:T(8,128)S(1)} fusion(bf16[3,3,320,320]{3,2,1,0:T(8,128)(2,1)} %reshape_reshape.15, bf16[34,1,7,2,320]{4,2,3,0,1:T(8,128)(2,1)} %slice.172, bf16[34,1,8,9,320]{4,2,3,0,1:T(8,128)(2,1)S(1)} %copy.10, pred[8,9]{0,1:T(8,128)(4,1)S(1)} %copy-done.20), kind=kOutput, calls=%fused_computation.109 | convolution fusion | flops 4253214720 | bytes 6663752 | tf_op jit(solution)/shard_map/conv_general_dilated | solution.py:85
  114.7 9.8 %all-reduce.10 = (f32[32]{0:T(128)S(1)}, f32[32]{0:T(128)S(1)}) all-reduce(f32[32]{0:T(128)S(1)} %reduce_sum.151, f32[32]{0:T(128)S(1)} %reduce_sum.149), channel_id=1, replica_groups=mesh['rows_0'=4,'rows_1'=4,'cols_0'=4,'cols_1'=2] {'rows_0'}, use_global_device_ids=true, to_apply=%region_20.21 | all-reduce | flops 64 | bytes 512 | tf_op jit(solution)/shard_map/psum | solution.py:19
  124.5 11.2 %all-reduce.6 = (f32[32]{0:T(128)S(1)}, f32[32]{0:T(128)S(1)}) all-reduce(f32[32]{0:T(128)S(1)} %get-tuple-element.47, f32[32]{0:T(128)S(1)} %get-tuple-element.48), channel_id=1, replica_groups=mesh['rows_0'=4,'rows_1'=4,'cols_0'=4,'cols_1'=2] {'rows_1'}, use_global_device_ids=true, to_apply=%region_21.22 | all-reduce | flops 64 | bytes 512 | tf_op jit(solution)/shard_map/psum | solution.py:19
  135.7 6.2 %all-reduce.2 = (f32[32]{0:T(128)S(1)}, f32[32]{0:T(128)S(1)}) all-reduce(f32[32]{0:T(128)S(1)} %get-tuple-element.39, f32[32]{0:T(128)S(1)} %get-tuple-element.40), channel_id=1, replica_groups=mesh['rows_0'=4,'rows_1'=4,'cols_0'=4,'cols_1'=2] {'cols_0'}, use_global_device_ids=true, to_apply=%region_22.23 | all-reduce | flops 64 | bytes 512 | tf_op jit(solution)/shard_map/psum | solution.py:19
  141.9 7.3 %all-reduce.14 = (f32[32]{0:T(128)S(1)}, f32[32]{0:T(128)S(1)}) all-reduce(f32[32]{0:T(128)S(1)} %get-tuple-element.31, f32[32]{0:T(128)S(1)} %get-tuple-element.32), channel_id=1, replica_groups=mesh['rows_0'=4,'rows_1'=4,'cols_0'=4,'cols_1'=2] {'cols_1'}, use_global_device_ids=true, to_apply=%region_23.24 | all-reduce | flops 64 | bytes 512 | tf_op jit(solution)/shard_map/psum | solution.py:19
  149.6 2.4 fusion.12
  152.2 2.1 collective-permute-start.4
  156.1 3.5 collective-permute-done.5
  159.7 3.7 collective-permute-start.6
  167.0 6.9 %all-to-all-start.2 = ((bf16[16,180,320]{2,1,0:T(8,128)(2,1)}), bf16[16,180,320]{2,1,0:T(8,128)(2,1)}, u32[]{:S(2)}, u32[]{:S(2)}) async-start(bf16[16,180,320]{2,1,0:T(8,128)(2,1)} %broadcast_in_dim.69), calls=%async_computation.2 | async-start | bytes 4521984 | tf_op jit(solution)/shard_map/all_to_all | solution.py:41
  173.9 4.2 %reshape_reshape.16 = bf16[3,3,320,320]{3,2,1,0:T(8,128)(2,1)} reshape(bf16[16,180,320]{2,1,0:T(8,128)(2,1)} %all-to-all-done.1) | data formatting | bytes 3686400 | tf_op jit(solution)/shard_map/reshape;reshape | solution.py:84
  182.0 8.0 %fusion.92 = f32[32,8,9,320]{3,1,2,0:T(8,128)S(1)} fusion(bf16[3,3,320,320]{3,2,1,0:T(8,128)(2,1)S(1)} %copy-done.3, bf16[34,1,7,2,320]{4,2,3,0,1:T(8,128)(2,1)S(1)} %slice.176, bf16[34,1,8,9,320]{4,2,3,0,1:T(8,128)(2,1)S(1)} %copy.13, pred[8,9]{0,1:T(8,128)(4,1)S(1)} %copy-done.21), kind=kOutput, calls=%fused_computation.108 | convolution fusion | flops 4253214720 | bytes 6663752 | tf_op jit(solution)/shard_map/conv_general_dilated | solution.py:85
  192.5 9.9 %all-reduce.9 = (f32[32]{0:T(128)S(1)}, f32[32]{0:T(128)S(1)}) all-reduce(f32[32]{0:T(128)S(1)} %reduce_sum.155, f32[32]{0:T(128)S(1)} %reduce_sum.153), channel_id=1, replica_groups=mesh['rows_0'=4,'rows_1'=4,'cols_0'=4,'cols_1'=2] {'rows_0'}, use_global_device_ids=true, to_apply=%region_32.33 | all-reduce | flops 64 | bytes 512 | tf_op jit(solution)/shard_map/psum | solution.py:19
  202.4 9.3 %all-reduce.5 = (f32[32]{0:T(128)S(1)}, f32[32]{0:T(128)S(1)}) all-reduce(f32[32]{0:T(128)S(1)} %get-tuple-element.45, f32[32]{0:T(128)S(1)} %get-tuple-element.46), channel_id=1, replica_groups=mesh['rows_0'=4,'rows_1'=4,'cols_0'=4,'cols_1'=2] {'rows_1'}, use_global_device_ids=true, to_apply=%region_33.34 | all-reduce | flops 64 | bytes 512 | tf_op jit(solution)/shard_map/psum | solution.py:19
  211.8 6.7 %all-reduce.1 = (f32[32]{0:T(128)S(1)}, f32[32]{0:T(128)S(1)}) all-reduce(f32[32]{0:T(128)S(1)} %get-tuple-element.37, f32[32]{0:T(128)S(1)} %get-tuple-element.38), channel_id=1, replica_groups=mesh['rows_0'=4,'rows_1'=4,'cols_0'=4,'cols_1'=2] {'cols_0'}, use_global_device_ids=true, to_apply=%region_34.35 | all-reduce | flops 64 | bytes 512 | tf_op jit(solution)/shard_map/psum | solution.py:19
  218.5 8.3 %all-reduce.13 = (f32[32]{0:T(128)S(1)}, f32[32]{0:T(128)S(1)}) all-reduce(f32[32]{0:T(128)S(1)} %get-tuple-element.29, f32[32]{0:T(128)S(1)} %get-tuple-element.30), channel_id=1, replica_groups=mesh['rows_0'=4,'rows_1'=4,'cols_0'=4,'cols_1'=2] {'cols_1'}, use_global_device_ids=true, to_apply=%region_35.36 | all-reduce | flops 64 | bytes 512 | tf_op jit(solution)/shard_map/psum | solution.py:19
  231.6 3.5 collective-permute-done.9
  235.2 3.6 collective-permute-start.10
  242.4 6.7 %all-to-all-start.3 = ((bf16[16,180,320]{2,1,0:T(8,128)(2,1)}), bf16[16,180,320]{2,1,0:T(8,128)(2,1)}, u32[]{:S(2)}, u32[]{:S(2)}) async-start(bf16[16,180,320]{2,1,0:T(8,128)(2,1)} %broadcast_in_dim.73), calls=%async_computation.3 | async-start | bytes 4521984 | tf_op jit(solution)/shard_map/all_to_all | solution.py:41
  249.2 4.2 %reshape_reshape.17 = bf16[3,3,320,320]{3,2,1,0:T(8,128)(2,1)} reshape(bf16[16,180,320]{2,1,0:T(8,128)(2,1)} %all-to-all-done.2) | data formatting | bytes 3686400 | tf_op jit(solution)/shard_map/reshape;reshape | solution.py:84
  257.3 8.0 %fusion.89 = f32[32,8,9,320]{3,1,2,0:T(8,128)S(1)} fusion(bf16[3,3,320,320]{3,2,1,0:T(8,128)(2,1)S(1)} %copy-done.4, bf16[34,1,7,2,320]{4,2,3,0,1:T(8,128)(2,1)S(1)} %slice.180, bf16[34,1,8,9,320]{4,2,3,0,1:T(8,128)(2,1)S(1)} %copy.16, pred[8,9]{0,1:T(8,128)(4,1)S(1)} %copy-done.22), kind=kOutput, calls=%fused_computation.107 | convolution fusion | flops 4253214720 | bytes 6663752 | tf_op jit(solution)/shard_map/conv_general_dilated | solution.py:85
  268.4 9.4 %all-reduce.8 = (f32[32]{0:T(128)S(1)}, f32[32]{0:T(128)S(1)}) all-reduce(f32[32]{0:T(128)S(1)} %reduce_sum.159, f32[32]{0:T(128)S(1)} %reduce_sum.157), channel_id=1, replica_groups=mesh['rows_0'=4,'rows_1'=4,'cols_0'=4,'cols_1'=2] {'rows_0'}, use_global_device_ids=true, to_apply=%region_44.45 | all-reduce | flops 64 | bytes 512 | tf_op jit(solution)/shard_map/psum | solution.py:19
  277.8 9.4 %all-reduce.4 = (f32[32]{0:T(128)S(1)}, f32[32]{0:T(128)S(1)}) all-reduce(f32[32]{0:T(128)S(1)} %get-tuple-element.43, f32[32]{0:T(128)S(1)} %get-tuple-element.44), channel_id=1, replica_groups=mesh['rows_0'=4,'rows_1'=4,'cols_0'=4,'cols_1'=2] {'rows_1'}, use_global_device_ids=true, to_apply=%region_45.46 | all-reduce | flops 64 | bytes 512 | tf_op jit(solution)/shard_map/psum | solution.py:19
  287.2 6.5 %all-reduce = (f32[32]{0:T(128)S(1)}, f32[32]{0:T(128)S(1)}) all-reduce(f32[32]{0:T(128)S(1)} %get-tuple-element.35, f32[32]{0:T(128)S(1)} %get-tuple-element.36), channel_id=1, replica_groups=mesh['rows_0'=4,'rows_1'=4,'cols_0'=4,'cols_1'=2] {'cols_0'}, use_global_device_ids=true, to_apply=%region_46.47 | all-reduce | flops 64 | bytes 512 | tf_op jit(solution)/shard_map/psum | solution.py:19
  293.7 8.6 %all-reduce.12 = (f32[32]{0:T(128)S(1)}, f32[32]{0:T(128)S(1)}) all-reduce(f32[32]{0:T(128)S(1)} %get-tuple-element.27, f32[32]{0:T(128)S(1)} %get-tuple-element.28), channel_id=1, replica_groups=mesh['rows_0'=4,'rows_1'=4,'cols_0'=4,'cols_1'=2] {'cols_1'}, use_global_device_ids=true, to_apply=%region_47.48 | all-reduce | flops 64 | bytes 512 | tf_op jit(solution)/shard_map/psum | solution.py:19
  302.7 2.4 fusion.21
  308.4 3.5 collective-permute-done.13
  312.0 3.8 collective-permute-start.14
  319.3 6.7 %all-to-all-start.4 = ((bf16[16,180,320]{2,1,0:T(8,128)(2,1)}), bf16[16,180,320]{2,1,0:T(8,128)(2,1)}, u32[]{:S(2)}, u32[]{:S(2)}) async-start(bf16[16,180,320]{2,1,0:T(8,128)(2,1)} %broadcast_in_dim.75), calls=%async_computation.4 | async-start | bytes 4521984 | tf_op jit(solution)/shard_map/all_to_all | solution.py:41
  326.1 4.2 %reshape_reshape.18 = bf16[3,3,320,320]{3,2,1,0:T(8,128)(2,1)} reshape(bf16[16,180,320]{2,1,0:T(8,128)(2,1)} %all-to-all-done.3) | data formatting | bytes 3686400 | tf_op jit(solution)/shard_map/reshape;reshape | solution.py:84
  334.2 8.0 %fusion.86 = f32[32,8,9,320]{3,1,2,0:T(8,128)S(1)} fusion(bf16[3,3,320,320]{3,2,1,0:T(8,128)(2,1)S(1)} %copy-done.2, bf16[34,1,7,2,320]{4,2,3,0,1:T(8,128)(2,1)S(1)} %slice.184, bf16[34,1,8,9,320]{4,2,3,0,1:T(8,128)(2,1)S(1)} %copy.19, pred[8,9]{0,1:T(8,128)(4,1)S(1)} %copy-done.22), kind=kOutput, calls=%fused_computation.106 | convolution fusion | flops 4253214720 | bytes 6663752 | tf_op jit(solution)/shard_map/conv_general_dilated | solution.py:85
  343.7 3.2 collective-permute-start.16
  348.3 10.9 %collective-permute-done.16 = bf16[1,64,320]{2,0,1:T(2,128)(2,1)S(1)} collective-permute-done((bf16[1,64,320]{2,0,1:T(2,128)(2,1)S(1)}, bf16[1,64,320]{2,0,1:T(2,128)(2,1)S(1)}, u32[]{:S(2)}, u32[]{:S(2)}) %collective-permute-start.16) | collective-permute-done | bytes 40992 | tf_op jit(solution)/shard_map/ppermute | solution.py:30
  359.2 3.4 collective-permute-done.17
  364.5 2.7 collective-permute-start.19
  367.2 4.1 %reshape_reshape.19 = bf16[3,3,320,320]{3,2,1,0:T(8,128)(2,1)} reshape(bf16[16,180,320]{2,1,0:T(8,128)(2,1)} %all-to-all-done.4) | data formatting | bytes 3686400 | tf_op jit(solution)/shard_map/reshape;reshape | solution.py:84
  376.1 2.2 fusion.98
  (172 shorter events, 68.6 us)
Async XLA Ops:
  2.6 9.3 %copy-start = (bf16[32,64,320]{2,1,0:T(8,128)(2,1)S(1)}, bf16[32,64,320]{2,1,0:T(8,128)(2,1)}, u32[]{:S(2)}) copy-start(bf16[32,64,320]{2,1,0:T(8,128)(2,1)} %param.6) | copy-start | bytes 3932164
  4.2 64.1 %copy-start.16 = (f32[4,320]{1,0:T(4,128)S(1)}, f32[4,320]{1,0:T(4,128)}, u32[]{:S(2)}) copy-start(f32[4,320]{1,0:T(4,128)} %param.9) | copy-start | bytes 15364
  4.2 64.7 %copy-start.17 = (f32[4,320]{1,0:T(4,128)S(1)}, f32[4,320]{1,0:T(4,128)}, u32[]{:S(2)}) copy-start(f32[4,320]{1,0:T(4,128)} %param.10) | copy-start | bytes 15364
  4.2 83.8 %all-to-all-start = ((bf16[16,180,320]{2,1,0:T(8,128)(2,1)}), bf16[16,180,320]{2,1,0:T(8,128)(2,1)}, u32[]{:S(2)}, u32[]{:S(2)}) async-start(bf16[16,180,320]{2,1,0:T(8,128)(2,1)} %broadcast_in_dim.61), calls=%async_computation | async-start | bytes 4521984 | tf_op jit(solution)/shard_map/all_to_all | solution.py:41
  12.9 69.8 %copy-start.18 = (f32[5,320]{1,0:T(8,128)S(1)}, f32[5,320]{1,0:T(8,128)}, u32[]{:S(2)}) copy-start(f32[5,320]{1,0:T(8,128)} %param.8) | copy-start | bytes 19204
  12.9 69.8 %copy-start.19 = (f32[2,320]{1,0:T(2,128)S(1)}, f32[2,320]{1,0:T(2,128)}, u32[]{:S(2)}) copy-start(f32[2,320]{1,0:T(2,128)} %param.11) | copy-start | bytes 7684
  71.1 3.4 collective-permute-start
  72.4 5.9 %collective-permute-start.1 = (bf16[1,64,320]{2,0,1:T(2,128)(2,1)S(1)}, bf16[1,64,320]{2,0,1:T(2,128)(2,1)S(1)}, u32[]{:S(2)}, u32[]{:S(2)}) collective-permute-start(bf16[1,64,320]{2,0,1:T(2,128)(2,1)S(1)} %get-tuple-element.81), channel_id=1, source_target_pairs={{8,0},{16,8},{24,16},{32,24},{40,32},{48,40},{56,48},{64,56},{72,6... | collective-permute-start | bytes 122888 | tf_op jit(solution)/shard_map/ppermute | solution.py:32
  78.3 5.0 %collective-permute-start.2 = (bf16[34,1,320]{2,0,1:T(8,128)(2,1)S(1)}, bf16[34,1,320]{2,0,1:T(8,128)(2,1)S(1)}, u32[]{:S(2)}, u32[]{:S(2)}) collective-permute-start(bf16[34,1,320]{2,0,1:T(8,128)(2,1)S(1)} %get-tuple-element.70), channel_id=1, source_target_pairs={{0,1},{1,2},{2,3},{3,4},{4,5},{5,6},{6,7},{8,9},{9,10},{10,11},{11... | collective-permute-start | bytes 65288 | tf_op jit(solution)/shard_map/ppermute | solution.py:30
  80.3 5.2 %collective-permute-start.3 = (bf16[34,1,320]{2,0,1:T(8,128)(2,1)S(1)}, bf16[34,1,320]{2,0,1:T(8,128)(2,1)S(1)}, u32[]{:S(2)}, u32[]{:S(2)}) collective-permute-start(bf16[34,1,320]{2,0,1:T(8,128)(2,1)S(1)} %get-tuple-element.71), channel_id=1, source_target_pairs={{1,0},{2,1},{3,2},{4,3},{5,4},{6,5},{7,6},{9,8},{10,9},{11,10},{12... | collective-permute-start | bytes 65288 | tf_op jit(solution)/shard_map/ppermute | solution.py:32
  90.5 74.8 %all-to-all-start.1 = ((bf16[16,180,320]{2,1,0:T(8,128)(2,1)}), bf16[16,180,320]{2,1,0:T(8,128)(2,1)}, u32[]{:S(2)}, u32[]{:S(2)}) async-start(bf16[16,180,320]{2,1,0:T(8,128)(2,1)} %broadcast_in_dim.65), calls=%async_computation.1 | async-start | bytes 4521984 | tf_op jit(solution)/shard_map/all_to_all | solution.py:41
  97.6 4.2 %copy-start.20 = (pred[8,9]{0,1:T(8,128)(4,1)S(1)}, pred[8,9]{0,1:T(8,128)(4,1)}, u32[]{:S(2)}) copy-start(pred[8,9]{0,1:T(8,128)(4,1)} %constant.41) | copy-start | bytes 220
  114.2 51.1 %copy-start.7 = (bf16[180,320]{1,0:T(8,128)(2,1)S(1)}, bf16[180,320]{1,0:T(8,128)(2,1)}, u32[]{:S(2)}) copy-start(bf16[180,320]{1,0:T(8,128)(2,1)} %get-tuple-element.83) | copy-start | bytes 345604
  152.2 3.9 %collective-permute-start.4 = (bf16[1,64,320]{2,0,1:T(2,128)(2,1)S(1)}, bf16[1,64,320]{2,0,1:T(2,128)(2,1)S(1)}, u32[]{:S(2)}, u32[]{:S(2)}) collective-permute-start(bf16[1,64,320]{2,0,1:T(2,128)(2,1)S(1)} %get-tuple-element.78), channel_id=1, source_target_pairs={{0,8},{8,16},{16,24},{24,32},{32,40},{40,48},{48,56},{56,64},{64,7... | collective-permute-start | bytes 122888 | tf_op jit(solution)/shard_map/ppermute | solution.py:30
  154.3 5.4 %collective-permute-start.5 = (bf16[1,64,320]{2,0,1:T(2,128)(2,1)S(1)}, bf16[1,64,320]{2,0,1:T(2,128)(2,1)S(1)}, u32[]{:S(2)}, u32[]{:S(2)}) collective-permute-start(bf16[1,64,320]{2,0,1:T(2,128)(2,1)S(1)} %get-tuple-element.79), channel_id=1, source_target_pairs={{8,0},{16,8},{24,16},{32,24},{40,32},{48,40},{56,48},{64,56},{72,6... | collective-permute-start | bytes 122888 | tf_op jit(solution)/shard_map/ppermute | solution.py:32
  159.7 18.4 %collective-permute-start.6 = (bf16[34,1,320]{2,0,1:T(8,128)(2,1)S(1)}, bf16[34,1,320]{2,0,1:T(8,128)(2,1)}, u32[]{:S(2)}, u32[]{:S(2)}) collective-permute-start(bf16[34,1,320]{2,0,1:T(8,128)(2,1)S(1)} %get-tuple-element.68), channel_id=1, source_target_pairs={{0,1},{1,2},{2,3},{3,4},{4,5},{5,6},{6,7},{8,9},{9,10},{10,11},{11... | collective-permute-start | bytes 65288 | tf_op jit(solution)/shard_map/ppermute | solution.py:30
  163.4 14.7 %collective-permute-start.7 = (bf16[34,1,320]{2,0,1:T(8,128)(2,1)S(1)}, bf16[34,1,320]{2,0,1:T(8,128)(2,1)}, u32[]{:S(2)}, u32[]{:S(2)}) collective-permute-start(bf16[34,1,320]{2,0,1:T(8,128)(2,1)S(1)} %get-tuple-element.69), channel_id=1, source_target_pairs={{1,0},{2,1},{3,2},{4,3},{5,4},{6,5},{7,6},{9,8},{10,9},{11,10},{12... | collective-permute-start | bytes 65288 | tf_op jit(solution)/shard_map/ppermute | solution.py:32
  167.0 73.8 %all-to-all-start.2 = ((bf16[16,180,320]{2,1,0:T(8,128)(2,1)}), bf16[16,180,320]{2,1,0:T(8,128)(2,1)}, u32[]{:S(2)}, u32[]{:S(2)}) async-start(bf16[16,180,320]{2,1,0:T(8,128)(2,1)} %broadcast_in_dim.69), calls=%async_computation.2 | async-start | bytes 4521984 | tf_op jit(solution)/shard_map/all_to_all | solution.py:41
  180.4 1.6 copy-start.3
  180.4 1.6 copy-start.21
  190.7 36.4 %copy-start.13 = (f32[320]{0:T(512)S(1)}, f32[320]{0:T(512)}, u32[]{:S(2)}) copy-start(f32[320]{0:T(512)} %get-tuple-element.20) | copy-start | bytes 3844
  190.7 36.5 %copy-start.15 = (f32[320]{0:T(512)S(1)}, f32[320]{0:T(512)}, u32[]{:S(2)}) copy-start(f32[320]{0:T(512)} %get-tuple-element.24) | copy-start | bytes 3844
  192.0 48.8 %copy-start.6 = (bf16[180,320]{1,0:T(8,128)(2,1)S(1)}, bf16[180,320]{1,0:T(8,128)(2,1)}, u32[]{:S(2)}) copy-start(bf16[180,320]{1,0:T(8,128)(2,1)} %get-tuple-element.86) | copy-start | bytes 345604
  228.4 3.3 collective-permute-start.8
  229.8 5.4 %collective-permute-start.9 = (bf16[1,64,320]{2,0,1:T(2,128)(2,1)S(1)}, bf16[1,64,320]{2,0,1:T(2,128)(2,1)S(1)}, u32[]{:S(2)}, u32[]{:S(2)}) collective-permute-start(bf16[1,64,320]{2,0,1:T(2,128)(2,1)S(1)} %get-tuple-element.77), channel_id=1, source_target_pairs={{8,0},{16,8},{24,16},{32,24},{40,32},{48,40},{56,48},{64,56},{72,6... | collective-permute-start | bytes 122888 | tf_op jit(solution)/shard_map/ppermute | solution.py:32
  235.2 18.2 %collective-permute-start.10 = (bf16[34,1,320]{2,0,1:T(8,128)(2,1)S(1)}, bf16[34,1,320]{2,0,1:T(8,128)(2,1)}, u32[]{:S(2)}, u32[]{:S(2)}) collective-permute-start(bf16[34,1,320]{2,0,1:T(8,128)(2,1)S(1)} %get-tuple-element.66), channel_id=1, source_target_pairs={{0,1},{1,2},{2,3},{3,4},{4,5},{5,6},{6,7},{8,9},{9,10},{10,11},{11... | collective-permute-start | bytes 65288 | tf_op jit(solution)/shard_map/ppermute | solution.py:30
  238.9 14.5 %collective-permute-start.11 = (bf16[34,1,320]{2,0,1:T(8,128)(2,1)S(1)}, bf16[34,1,320]{2,0,1:T(8,128)(2,1)}, u32[]{:S(2)}, u32[]{:S(2)}) collective-permute-start(bf16[34,1,320]{2,0,1:T(8,128)(2,1)S(1)} %get-tuple-element.67), channel_id=1, source_target_pairs={{1,0},{2,1},{3,2},{4,3},{5,4},{6,5},{7,6},{9,8},{10,9},{11,10},{12... | collective-permute-start | bytes 65288 | tf_op jit(solution)/shard_map/ppermute | solution.py:32
  242.4 75.3 %all-to-all-start.3 = ((bf16[16,180,320]{2,1,0:T(8,128)(2,1)}), bf16[16,180,320]{2,1,0:T(8,128)(2,1)}, u32[]{:S(2)}, u32[]{:S(2)}) async-start(bf16[16,180,320]{2,1,0:T(8,128)(2,1)} %broadcast_in_dim.73), calls=%async_computation.3 | async-start | bytes 4521984 | tf_op jit(solution)/shard_map/all_to_all | solution.py:41
  255.6 1.6 copy-start.4
  255.7 1.6 copy-start.22
  265.3 0.7 copy-start.10
  265.3 0.7 copy-start.11
  266.0 36.6 %copy-start.12 = (f32[320]{0:T(512)S(1)}, f32[320]{0:T(512)}, u32[]{:S(2)}) copy-start(f32[320]{0:T(512)} %get-tuple-element.17) | copy-start | bytes 3844
  266.0 36.7 %copy-start.14 = (f32[320]{0:T(512)S(1)}, f32[320]{0:T(512)}, u32[]{:S(2)}) copy-start(f32[320]{0:T(512)} %get-tuple-element.21) | copy-start | bytes 3844
  268.0 49.7 %copy-start.5 = (bf16[180,320]{1,0:T(8,128)(2,1)S(1)}, bf16[180,320]{1,0:T(8,128)(2,1)}, u32[]{:S(2)}) copy-start(bf16[180,320]{1,0:T(8,128)(2,1)} %get-tuple-element.82) | copy-start | bytes 345604
  305.3 3.1 collective-permute-start.12
  306.6 5.4 %collective-permute-start.13 = (bf16[1,64,320]{2,0,1:T(2,128)(2,1)S(1)}, bf16[1,64,320]{2,0,1:T(2,128)(2,1)S(1)}, u32[]{:S(2)}, u32[]{:S(2)}) collective-permute-start(bf16[1,64,320]{2,0,1:T(2,128)(2,1)S(1)} %get-tuple-element.75), channel_id=1, source_target_pairs={{8,0},{16,8},{24,16},{32,24},{40,32},{48,40},{56,48},{64,56},{72,6... | collective-permute-start | bytes 122888 | tf_op jit(solution)/shard_map/ppermute | solution.py:32
  312.0 18.3 %collective-permute-start.14 = (bf16[34,1,320]{2,0,1:T(8,128)(2,1)S(1)}, bf16[34,1,320]{2,0,1:T(8,128)(2,1)}, u32[]{:S(2)}, u32[]{:S(2)}) collective-permute-start(bf16[34,1,320]{2,0,1:T(8,128)(2,1)S(1)} %get-tuple-element.64), channel_id=1, source_target_pairs={{0,1},{1,2},{2,3},{3,4},{4,5},{5,6},{6,7},{8,9},{9,10},{10,11},{11... | collective-permute-start | bytes 65288 | tf_op jit(solution)/shard_map/ppermute | solution.py:30
  315.8 14.5 %collective-permute-start.15 = (bf16[34,1,320]{2,0,1:T(8,128)(2,1)S(1)}, bf16[34,1,320]{2,0,1:T(8,128)(2,1)}, u32[]{:S(2)}, u32[]{:S(2)}) collective-permute-start(bf16[34,1,320]{2,0,1:T(8,128)(2,1)S(1)} %get-tuple-element.65), channel_id=1, source_target_pairs={{1,0},{2,1},{3,2},{4,3},{5,4},{6,5},{7,6},{9,8},{10,9},{11,10},{12... | collective-permute-start | bytes 65288 | tf_op jit(solution)/shard_map/ppermute | solution.py:32
  319.3 47.9 %all-to-all-start.4 = ((bf16[16,180,320]{2,1,0:T(8,128)(2,1)}), bf16[16,180,320]{2,1,0:T(8,128)(2,1)}, u32[]{:S(2)}, u32[]{:S(2)}) async-start(bf16[16,180,320]{2,1,0:T(8,128)(2,1)} %broadcast_in_dim.75), calls=%async_computation.4 | async-start | bytes 4521984 | tf_op jit(solution)/shard_map/all_to_all | solution.py:41
  332.5 1.6 copy-start.2
  343.7 15.4 %collective-permute-start.16 = (bf16[1,64,320]{2,0,1:T(2,128)(2,1)S(1)}, bf16[1,64,320]{2,0,1:T(2,128)(2,1)S(1)}, u32[]{:S(2)}, u32[]{:S(2)}) collective-permute-start(bf16[1,64,320]{2,0,1:T(2,128)(2,1)S(1)} %get-tuple-element.72), channel_id=1, source_target_pairs={{0,8},{8,16},{16,24},{24,32},{32,40},{40,48},{48,56},{56,64},{64,7... | collective-permute-start | bytes 122888 | tf_op jit(solution)/shard_map/ppermute | solution.py:30
  347.0 15.6 %collective-permute-start.17 = (bf16[1,64,320]{2,0,1:T(2,128)(2,1)S(1)}, bf16[1,64,320]{2,0,1:T(2,128)(2,1)S(1)}, u32[]{:S(2)}, u32[]{:S(2)}) collective-permute-start(bf16[1,64,320]{2,0,1:T(2,128)(2,1)S(1)} %get-tuple-element.73), channel_id=1, source_target_pairs={{8,0},{16,8},{24,16},{32,24},{40,32},{48,40},{56,48},{64,56},{72,6... | collective-permute-start | bytes 122888 | tf_op jit(solution)/shard_map/ppermute | solution.py:32
  362.6 10.4 %collective-permute-start.18 = (bf16[34,1,320]{2,0,1:T(8,128)(2,1)S(1)}, bf16[34,1,320]{2,0,1:T(8,128)(2,1)S(1)}, u32[]{:S(2)}, u32[]{:S(2)}) collective-permute-start(bf16[34,1,320]{2,0,1:T(8,128)(2,1)S(1)} %get-tuple-element.62), channel_id=1, source_target_pairs={{0,1},{1,2},{2,3},{3,4},{4,5},{5,6},{6,7},{8,9},{9,10},{10,11},{11... | collective-permute-start | bytes 65288 | tf_op jit(solution)/shard_map/ppermute | solution.py:30
  364.5 8.5 %collective-permute-start.19 = (bf16[34,1,320]{2,0,1:T(8,128)(2,1)S(1)}, bf16[34,1,320]{2,0,1:T(8,128)(2,1)S(1)}, u32[]{:S(2)}, u32[]{:S(2)}) collective-permute-start(bf16[34,1,320]{2,0,1:T(8,128)(2,1)S(1)} %get-tuple-element.63), channel_id=1, source_target_pairs={{1,0},{2,1},{3,2},{4,3},{5,4},{6,5},{7,6},{9,8},{10,9},{11,10},{12... | collective-permute-start | bytes 65288 | tf_op jit(solution)/shard_map/ppermute | solution.py:32
  374.5 1.6 copy-start.1
  374.5 1.6 copy-start.23
  376.1 2.4 copy-start.8
  (1 other events, 0.7 us)
where the time goes:
time: 387 us; the launch traced here: 380 us
  blocking collectives  157 us (41%)
  starting transfers between devices  77 us (20%)
  local copies, waits for them, and re-layouts  51.1 us (13%)
  matrix products  36 us (9%)
  waiting for transfers between devices  33.2 us (9%)
  other arithmetic  23.3 us (6%)
    psum x16, blocking collectives, by_axis(): return functools.reduce(lax.psum, axes, value)  157 us
    conv_general_dilated x5, matrix products, conv_local(): lax.conv_general_dilated(padded[None], kernel, (stride, stride), 'VALID',...  36 us
    all_to_all x5, starting transfers between devices, from_everyone(): return lax.all_to_all(copies, axis, split_axis=0, concat_axis=0, tiled=True)  35.3 us
    ppermute x10, starting transfers between devices, extended(): lax.ppermute(tail, axis, [(i, (i + 1) % count) for i in range(ends)])  24.3 us
    another operation x5, local copies, waits for them, and re-layouts, conv_local(): kernel = kernel_rows.reshape(3, 3, width_in, kernel_rows.shape[1])  21 us
    ppermute x10, waiting for transfers between devices, extended(): lax.ppermute(head, axis, [((i + 1) % count, i) for i in range(ends)])  19.9 us
    ppermute x10, starting transfers between devices, extended(): lax.ppermute(head, axis, [((i + 1) % count, i) for i in range(ends)])  17.3 us
    ppermute x10, waiting for transfers between devices, extended(): lax.ppermute(tail, axis, [(i, (i + 1) % count) for i in range(ends)])  13.3 us
  transfers between devices with their start and end apart: 25, of which 11 were waited for; matrix products, arithmetic and copies ran while one was open for 25% of the time, Pallas kernels for 0%

commit v1 on v0

v1 whole, which is shorter than its diff:
```python
import functools

import jax
import jax.numpy as jnp
from jax import lax
from jax.experimental import pallas as pl
from jax.experimental.pallas import tpu as pltpu
from jax.sharding import Mesh
from jax.sharding import PartitionSpec as P

f32, bf16 = jnp.float32, jnp.bfloat16
MESH = pl.DeviceIdType.MESH
ROWS = ("rows_0", "rows_1")
COLS = ("cols_0", "cols_1")
NY, NX, NZ, NC = 4, 4, 4, 2
NR, NCOL = NY * NX, NZ * NC
C = 320
TH, TW = 32, 64
SHARD = 180
RB = 16
EPS = 1e-05


def padded(row, width=384):
    return jnp.concatenate([row, jnp.zeros((row.shape[0], width - row.shape[1]), row.dtype)], axis=1)


def window_tiles():
    tiles = []
    for tile in range(9 * C // 16):
        holders = []
        for r in range(NR):
            first = SHARD * r // 16
            last = (SHARD * (r + 1) - 1) // 16
            if first <= tile <= last:
                holders.append((r, tile - first))
        tiles.append(holders)
    return tiles


WINDOWS = window_tiles()


def kernel(
    lat_hbm, w_hbm, bias_ref, gain_ref, shift_ref, time_ref,
    feat_hbm, red_hbm,
    lat, wl, act_a, act_b, xs, r0, edge_mat, zs, ze, hc, es, cs, gath, wk, blockdiag,
    ar_src, ar_a, ar_b, fbuf, rbuf,
    sem_in, sem_out, ws_send, ws_recv, halo_send, halo_recv, ar_send, ar_recv,
):
    y, x = lax.axis_index("rows_0"), lax.axis_index("rows_1")
    z, core = lax.axis_index("cols_0"), lax.axis_index("cols_1")
    r, c = y * NX + x, z * NC + core

    def dev(rr, cc):
        return (rr // NX, lax.rem(rr, NX), cc // NC, lax.rem(cc, NC))

    def row_peer(j):
        return dev(lax.rem(r + j, NR), c)

    def col_peer(j):
        return dev(r, lax.rem(c + j, NCOL))

    up, down = lax.rem(r + NR - 1, NR), lax.rem(r + 1, NR)
    left, right = lax.rem(c + NCOL - 1, NCOL), lax.rem(c + 1, NCOL)

    lat_copies = []
    for i in range(4):
        cp = pltpu.make_async_copy(lat_hbm.at[pl.ds(8 * i, 8)], lat.at[pl.ds(8 * i, 8)], sem_in.at[i])
        cp.start()
        lat_copies.append(cp)
    w_copy = pltpu.make_async_copy(w_hbm, wl, sem_in.at[4])
    w_copy.start()

    barrier = pltpu.get_barrier_semaphore()
    peers = [row_peer(j) for j in range(1, NR)] + [col_peer(j) for j in range(1, NCOL)]
    peers += [dev(up, left), dev(up, right), dev(down, left), dev(down, right)]
    for peer in peers:
        pl.semaphore_signal(barrier, inc=1, device_id=peer, device_id_type=MESH)

    major = jnp.where(core == 0, y, x)
    minor = jnp.where(core == 0, x, y)
    slot = 4 * major + minor
    w_copy.wait()
    off = lax.rem(4 * r, 16)
    row_id = lax.broadcasted_iota(jnp.int32, (96, SHARD), 0) + 96 * core
    col_id = lax.broadcasted_iota(jnp.int32, (96, SHARD), 1) + off
    place = jnp.where(row_id == col_id, 1.0, 0.0).astype(bf16)
    for k in range(5):
        half = jnp.dot(place, wl[k], preferred_element_type=f32)
        gath[k, core, slot, 0:96] = half[:, 0:128].astype(bf16)
        gath[k, core, slot, 96:192] = half[:, 128:256].astype(bf16)
        tail = jnp.concatenate([half[0:48, 256:320], half[48:96, 256:320]], axis=1)
        gath[k, core, slot, 192:240] = tail.astype(bf16)

    pl.semaphore_wait(barrier, len(peers))

    def along(step_minor, step_major):
        mi = lax.rem(minor + step_minor, 4)
        ma = lax.rem(major + step_major, 4)
        return (jnp.where(core == 0, ma, mi), jnp.where(core == 0, mi, ma), z, core)

    pending_sends = []

    def w_stage1(k):
        mine = gath.at[k, core, slot]
        for j in range(1, 4):
            pltpu.make_async_remote_copy(mine, mine, ws_send.at[k, 0], ws_recv.at[k, 0], along(j, 0), MESH).start()
        pending_sends.append((gath.at[k, 0, 0:3], ws_send.at[k, 0]))

    def w_stage2(k):
        three = gath.at[k, 0, 0:3]
        pltpu.make_async_copy(three, three, ws_recv.at[k, 0]).wait()
        mine = gath.at[k, core, pl.ds(4 * major, 4)]
        for j in range(1, 4):
            pltpu.make_async_remote_copy(mine, mine, ws_send.at[k, 1], ws_recv.at[k, 1], along(0, j), MESH).start()
        pending_sends.append((gath.at[k, 0, 0:12], ws_send.at[k, 1]))

    def w_swap(k):
        twelve = gath.at[k, 0, 0:12]
        pltpu.make_async_copy(twelve, twelve, ws_recv.at[k, 1]).wait()
        mine = gath.at[k, core]
        pltpu.make_async_remote_copy(
            mine, mine, ws_send.at[k, 2], ws_recv.at[k, 2], (y, x, z, 1 - core), MESH
        ).start()
        pending_sends.append((gath.at[k, 0], ws_send.at[k, 2]))

    def w_arrived(k):
        every = gath.at[k, 0]
        pltpu.make_async_copy(every, every, ws_recv.at[k, 2]).wait()

    w_stage1(0)

    lane = lax.broadcasted_iota(jnp.int32, (1, 128), 1)
    low = lane < 64

    def relayout(k):
        wbuf = wk.at[k % 2]

        def piece(holder, part):
            rr, l = holder
            h, l6 = l // 6, l % 6
            s = rr if h == 0 else (rr % NX) * NY + rr // NX
            if part < 2:
                return gath[k, h, s, 96 * part + 16 * l6 : 96 * part + 16 * l6 + 16]
            t = gath[k, h, s, 192 + 16 * (l6 % 3) : 208 + 16 * (l6 % 3)].astype(f32)
            return t if l6 < 3 else pltpu.roll(t, 64, 1)

        def tile(t, part):
            return functools.reduce(lambda p, q: p + q, [piece(h, part) for h in WINDOWS[t]])

        for a in range(3):
            for u in range(20):
                row = 256 * a + 16 * u if u < 16 else 768 + 64 * a + 16 * (u - 16)
                tails = []
                for b in range(3):
                    t = 20 * (3 * a + b) + u
                    for part in range(2):
                        wbuf[row : row + 16, 256 * b + 128 * part : 256 * b + 128 * part + 128] = tile(t, part)
                    tails.append(jnp.where(low, tile(t, 2), 0.0))
                wbuf[row : row + 16, 768:896] = (tails[0] + pltpu.roll(tails[1], 64, 1)).astype(bf16)
                wbuf[row : row + 16, 896:1024] = tails[2].astype(bf16)

    for i in range(2):
        wk[i, 960:1024, :] = jnp.zeros((64, 1024), bf16)
    ci = lax.broadcasted_iota(jnp.int32, (384, 384), 0)
    cj = lax.broadcasted_iota(jnp.int32, (384, 384), 1)
    same = ((ci * 6554) >> 16) == ((cj * 6554) >> 16)
    blockdiag[...] = jnp.where(same, 1.0, 0.0).astype(bf16)

    zero_acc = tuple(jnp.zeros((8, 128), f32) for _ in range(6))

    def fold(v):
        return jnp.sum(v.reshape(v.shape[0] // 8, 8, 128), axis=0)

    def add_stats(acc, tiles):
        sums = [acc[t] + fold(tiles[t]) for t in range(3)]
        squares = [acc[3 + t] + fold(tiles[t] * tiles[t]) for t in range(3)]
        return tuple(sums + squares)

    def stage_cols(phase, row, tiles):
        for t in range(3):
            cs[phase, 0, t, pl.ds(row, 1), :] = tiles[t][0:1]
            cs[phase, 1, t, pl.ds(row, 1), :] = tiles[t][63:64]

    def halo_messages(phase, act):
        msgs = [
            (act.at[TH], act.at[0], dev(down, c)),
            (cs.at[phase, 1], hc.at[phase, 0, :, 8:40, :], dev(r, right)),
            (cs.at[phase, 1, :, 24:32, :], hc.at[phase, 0, :, 0:8, :], dev(down, right)),
        ]
        if phase < 4:
            msgs += [
                (act.at[1], act.at[TH + 1], dev(up, c)),
                (cs.at[phase, 0], hc.at[phase, 1, :, 8:40, :], dev(r, left)),
                (cs.at[phase, 0, :, 24:32, :], hc.at[phase, 1, :, 0:8, :], dev(down, left)),
                (cs.at[phase, 1, :, 0:8, :], hc.at[phase, 0, :, 40:48, :], dev(up, right)),
                (cs.at[phase, 0, :, 0:8, :], hc.at[phase, 1, :, 40:48, :], dev(up, left)),
            ]
        return [
            pltpu.make_async_remote_copy(s, d, halo_send.at[phase, i], halo_recv.at[phase, i], to, MESH)
            for i, (s, d, to) in enumerate(msgs)
        ]

    def all_sum(phase, acc, between):
        vec = jnp.concatenate(
            [jnp.sum(v, axis=0, keepdims=True) for v in acc] + [jnp.zeros((2, 128), f32)], axis=0
        )
        for stage, (buf, peer, n) in enumerate(((ar_a, col_peer, NCOL), (ar_b, row_peer, NR))):
            src = ar_src.at[phase, stage]
            src[...] = vec
            for j in range(1, n):
                pltpu.make_async_remote_copy(
                    src, buf.at[phase, j - 1], ar_send.at[phase, stage], ar_recv.at[phase, stage], peer(j), MESH
                ).start()
            pending_sends.append((buf.at[phase], ar_send.at[phase, stage]))
            between[stage]()
            pltpu.make_async_copy(buf.at[phase], buf.at[phase], ar_recv.at[phase, stage]).wait()
            vec = functools.reduce(lambda p, q: p + q, [vec] + [buf[phase, j] for j in range(n - 1)])
        return vec

    def scales(phase, vec):
        both = jnp.concatenate(
            [
                jnp.concatenate([vec[0:1], vec[1:2], vec[2:3]], axis=1),
                jnp.concatenate([vec[3:4], vec[4:5], vec[5:6]], axis=1),
            ],
            axis=0,
        )
        hi = both.astype(bf16).astype(f32)
        mid = (both - hi).astype(bf16).astype(f32)
        lo = both - hi - mid
        parts = jnp.concatenate([hi, mid, lo, jnp.zeros((10, 384), f32)], axis=0).astype(bf16)
        tot = jnp.dot(parts, blockdiag[...], preferred_element_type=f32)
        sums = tot[0:1] + tot[2:3] + tot[4:5]
        squares = tot[1:2] + tot[3:4] + tot[5:6]
        count = float(TH * NR * TW * NCOL * (C // 32))
        mean = sums / count
        spread = jnp.maximum(squares / count - mean * mean, 0.0)
        scale = lax.rsqrt(spread + EPS) * padded(gain_ref[phase : phase + 1, :])
        move = padded(shift_ref[phase : phase + 1, :]) - mean * scale
        scale, move = 0.5 * scale, 0.5 * move
        return [scale[:, 128 * t : 128 * t + 128] for t in range(3)], [move[:, 128 * t : 128 * t + 128] for t in range(3)]

    def silu_of(v, scale, move):
        half = v * scale + move
        return half + half * jnp.tanh(half)

    def on(cond):
        return jnp.where(cond, 1.0, 0.0).astype(f32)

    top, bottom = on(r > 0), on(r < NR - 1)
    west, east = on(c > 0), on(c < NCOL - 1)

    def edges_to_matrix(rows, stride, sides):
        for side in range(sides):
            at = slice(rows * side, rows * side + rows)
            taps = [
                [es[side, t, pl.ds(7 + a, rows, stride=stride) if stride > 1 else pl.ds(7 + a, rows), :] for t in range(3)]
                for a in range(3)
            ]
            for a in range(3):
                for t in range(2):
                    edge_mat[at, 256 * a + 128 * t : 256 * a + 128 * t + 128] = taps[a][t].astype(bf16)
            edge_mat[at, 768:896] = (taps[0][2] + pltpu.roll(taps[1][2], 64, 1)).astype(bf16)
            edge_mat[at, 896:1024] = taps[2][2].astype(bf16)

    er = lax.broadcasted_iota(jnp.int32, (48, 1), 0)
    edge_rows = jnp.where(er < 8, top, jnp.where(er < 40, 1.0, bottom))

    def normalize(phase, act, sc, mv):
        def one(i, prev):
            m = jnp.where(i == 0, top, jnp.where(i == TH + 1, bottom, 1.0))
            tiles = []
            for t in range(3):
                v = act[i, :, 128 * t : 128 * t + 128].astype(f32)
                tiles.append(silu_of(v, sc[t] * m, mv[t] * m))
                xs[i, :, 128 * t : 128 * t + 128] = tiles[t].astype(bf16)
            r0[i, :, :] = (prev + pltpu.roll(tiles[2], 64, 1)).astype(bf16)
            return tiles[2]

        lax.fori_loop(0, TH + 2, one, jnp.zeros((TW, 128), f32))
        for side, mask in ((0, west), (1, east)):
            for t in range(3):
                es[side, t] = silu_of(hc[phase, side, t], sc[t], mv[t]) * (edge_rows * mask)
        edges_to_matrix(TH, 1, 2)

    def edge_dot(k, rows):
        for n in range(4):
            o = jnp.dot(edge_mat[0:rows], wk[k % 2, :, 256 * n : 256 * n + 256], preferred_element_type=f32)
            ze[2 * n, 0:rows] = o[:, 0:128]
            ze[2 * n + 1, 0:rows] = o[:, 128:256]

    def block_dot(k, parts):
        lhs = jnp.concatenate(parts, axis=1)
        for n in range(4):
            o = jnp.dot(lhs, wk[k % 2, :, 256 * n : 256 * n + 256], preferred_element_type=f32)
            zs[2 * n, :, 8 : 8 + TW, :] = o[:, 0:128].reshape(RB, TW, 128)
            zs[2 * n + 1, :, 8 : 8 + TW, :] = o[:, 128:256].reshape(RB, TW, 128)

    def taps_sum(rr, width, stride):
        def at(t, first):
            if stride > 1:
                return zs[t, rr, pl.ds(first, width, stride=stride), :]
            return zs[t, rr, first : first + width, :]

        outs = [at(t, 7) + at(2 + t, 8) + at(4 + t, 9) for t in range(2)]
        tail = at(6, 7) + pltpu.roll(at(6, 8), 64, 1) + at(7, 9)
        return outs + [jnp.where(low, tail, 0.0)]

    def place_edges(rr, row, rows, both):
        for t in (0, 1, 6):
            zs[t, rr, 7:8, :] = ze[t, pl.ds(row, 1), :]
        if both:
            for t in (4, 5, 7):
                zs[t, rr, 72:73, :] = ze[t, pl.ds(rows + row, 1), :]

    def split(row):
        row = padded(row)
        return [row[:, 128 * t : 128 * t + 128] for t in range(3)]

    def convolve(k, res, out):
        extra = split(bias_ref[k : k + 1, :] + (time_ref[k // 2 : k // 2 + 1, :] if k % 2 == 0 else 0.0))
        edge_dot(k, 2 * TH)

        def block(i, acc):
            first = i * RB
            parts = [xs[pl.ds(first + a, RB), :, 0:256].reshape(RB * TW, 256) for a in range(3)]
            parts.append(r0[pl.ds(first + 1, RB)].reshape(RB * TW, 128))
            parts.append(xs[pl.ds(first + 2, RB), :, 256:384].reshape(RB * TW, 128))
            block_dot(k, parts)

            def one(rr, acc):
                row = first + rr
                place_edges(rr, row, TH, True)
                tiles = []
                for t, o in enumerate(taps_sum(rr, TW, 1)):
                    o = o + extra[t]
                    if res is not None:
                        o = o + res[row + 1, :, 128 * t : 128 * t + 128].astype(f32)
                    o = o.astype(bf16)
                    out[row + 1, :, 128 * t : 128 * t + 128] = o
                    tiles.append(o.astype(f32))
                stage_cols(k + 1, row, tiles)
                if k == 3:
                    fbuf[row] = jnp.concatenate([tiles[0], tiles[1], tiles[2][:, 0:64]], axis=1).astype(bf16)
                    return acc
                return add_stats(acc, tiles)

            return lax.fori_loop(0, RB, one, acc)

        return lax.fori_loop(0, TH // RB, block, zero_acc)

    def read_latent(i, acc):
        v = lat[i].astype(f32)
        tiles = [v[:, 0:128], v[:, 128:256], padded(v[:, 256:320], 128)]
        for t in range(3):
            act_a[i + 1, :, 128 * t : 128 * t + 128] = tiles[t].astype(bf16)
        stage_cols(0, i, tiles)
        return add_stats(acc, tiles)

    acc = zero_acc
    for i in range(4):
        lat_copies[i].wait()
        acc = lax.fori_loop(8 * i, 8 * i + 8, read_latent, acc)

    def nothing():
        pass

    for k in range(4):
        act, res, out = (act_a, None, act_b) if k % 2 == 0 else (act_b, act_a, act_a)
        halos = halo_messages(k, act)
        for h in halos:
            h.start()
        if k == 0:
            def first_wait():
                w_stage2(0)
                w_stage1(1)

            def second_wait():
                w_swap(0)
                w_stage2(1)
                w_arrived(0)
                relayout(0)
        else:
            def first_wait(k=k):
                w_arrived(k)
                w_stage2(k + 1)

            def second_wait(k=k):
                relayout(k)
        vec = all_sum(k, acc, (first_wait, second_wait))
        sc, mv = scales(k, vec)
        for h in halos:
            h.wait()
        w_swap(k + 1)
        if k < 3:
            w_stage1(k + 2)
        normalize(k, act, sc, mv)
        acc = convolve(k, res, out)

    halos = halo_messages(4, act_a)
    for h in halos:
        h.start()
    feat_copy = pltpu.make_async_copy(fbuf, feat_hbm, sem_out.at[0])
    feat_copy.start()
    w_arrived(4)
    relayout(4)
    for h in halos:
        h.wait()
    for t in range(3):
        act_a[0, :, 128 * t : 128 * t + 128] = (act_a[0, :, 128 * t : 128 * t + 128].astype(f32) * top).astype(bf16)
        es[0, t] = hc[4, 0, t] * (edge_rows * west)
    edges_to_matrix(TH // 2, 2, 1)

    def tails4(p, carry):
        pair = act_a[2 * p, :, 256:384].astype(f32) + pltpu.roll(act_a[2 * p + 1, :, 256:384].astype(f32), 64, 1)
        r0[p, :, :] = pair.astype(bf16)
        return carry

    lax.fori_loop(0, TH // 2, tails4, 0)
    edge_dot(4, TH // 2)
    half = TH // 2

    def every_other(first, lanes):
        return jnp.concatenate([act_a[2 * p + first, :, lanes] for p in range(half)], axis=0)

    parts = [every_other(a, slice(0, 256)) for a in range(3)]
    parts.append(r0[0:half].reshape(half * TW, 128))
    parts.append(every_other(2, slice(256, 384)))
    block_dot(4, parts)
    extra4 = split(bias_ref[4:5, :])

    def last(p, carry):
        place_edges(p, p, half, False)
        tiles = [o + extra4[t] for t, o in enumerate(taps_sum(p, TW // 2, 2))]
        rbuf[p] = jnp.concatenate([tiles[0], tiles[1], tiles[2][:, 0:64]], axis=1).astype(bf16)
        return carry

    lax.fori_loop(0, half, last, 0)
    red_copy = pltpu.make_async_copy(rbuf, red_hbm, sem_out.at[1])
    red_copy.start()
    for ref, sem in pending_sends:
        pltpu.make_async_copy(ref, ref, sem).wait()
    feat_copy.wait()
    red_copy.wait()


def local(latent, conv_weights, conv_bias, norm_gain, norm_shift, time_shift):
    vmem, anywhere = pl.BlockSpec(memory_space=pltpu.VMEM), pl.BlockSpec(memory_space=pl.ANY)
    return pl.pallas_call(
        kernel,
        out_shape=(
            jax.ShapeDtypeStruct((TH, TW, C), bf16),
            jax.ShapeDtypeStruct((TH // 2, TW // 2, C), bf16),
        ),
        in_specs=[anywhere, anywhere, vmem, vmem, vmem, vmem],
        out_specs=(anywhere, anywhere),
        scratch_shapes=[
            pltpu.VMEM((TH, TW, C), bf16),
            pltpu.VMEM((5, SHARD, C), bf16),
            pltpu.VMEM((TH + 2, TW, 384), bf16),
            pltpu.VMEM((TH + 2, TW, 384), bf16),
            pltpu.VMEM((TH + 2, TW, 384), bf16),
            pltpu.VMEM((TH + 2, TW, 128), bf16),
            pltpu.VMEM((2 * TH, 1024), bf16),
            pltpu.VMEM((8, RB, 80, 128), f32),
            pltpu.VMEM((8, 2 * TH, 128), f32),
            pltpu.VMEM((5, 2, 3, 48, 128), f32),
            pltpu.VMEM((2, 3, 48, 128), f32),
            pltpu.VMEM((5, 2, 3, TH, 128), f32),
            pltpu.VMEM((5, 2, NR, 240, 128), bf16),
            pltpu.VMEM((2, 1024, 1024), bf16),
            pltpu.VMEM((384, 384), bf16),
            pltpu.VMEM((4, 2, 8, 128), f32),
            pltpu.VMEM((4, NCOL - 1, 8, 128), f32),
            pltpu.VMEM((4, NR - 1, 8, 128), f32),
            pltpu.VMEM((TH, TW, C), bf16),
            pltpu.VMEM((TH // 2, TW // 2, C), bf16),
            pltpu.SemaphoreType.DMA((5,)),
            pltpu.SemaphoreType.DMA((2,)),
            pltpu.SemaphoreType.DMA((5, 3)),
            pltpu.SemaphoreType.DMA((5, 3)),
            pltpu.SemaphoreType.DMA((5, 8)),
            pltpu.SemaphoreType.DMA((5, 8)),
            pltpu.SemaphoreType.DMA((4, 2)),
            pltpu.SemaphoreType.DMA((4, 2)),
        ],
        compiler_params=pltpu.CompilerParams(
            collective_id=0, has_side_effects=True, vmem_limit_bytes=60 * 1024 * 1024
        ),
        name="down_block",
    )(latent, conv_weights, conv_bias, norm_gain, norm_shift, time_shift)


def solution(mesh):
    split = Mesh(mesh.devices.reshape(NY, NX, NZ, NC), ("rows_0", "rows_1", "cols_0", "cols_1"))
    placed = (P(ROWS, COLS, None), P(None, ROWS, None), P(), P(), P(), P())
    return jax.shard_map(
        local,
        mesh=split,
        in_specs=placed,
        out_specs=(P(ROWS, COLS, None), P(ROWS, COLS, None)),
        check_vma=False,
    )
```

time: 387 us -> 127 us (0.33); the launches traced: 380 us -> 126 us
  blocking collectives: 157 us -> 0 us
  Pallas kernels: 0 us -> 122 us
  starting transfers between devices: 77 us -> 0 us
  local copies, waits for them, and re-layouts: 51.1 us -> 3.51 us
  matrix products: 36 us -> 0 us
  waiting for transfers between devices: 33.2 us -> 0 us
  other arithmetic: 23.3 us -> 0 us
    psum x16 -> x0, blocking collectives: 157 us -> none  [by_axis(): return functools.reduce(lax.psum, axes, value)]
    pallas_call x0 -> x1, Pallas kernels: none -> 122 us  [local(): pl.pallas_call(kernel, out_shape=(jax.ShapeDtypeStruct((TH, TW, C), bf16)...]
    ppermute x20 -> x0, starting transfers between devices: 41.7 us -> none  [the longest x10 24.3 us: extended(): lax.ppermute(tail, axis, [(i, (i + 1) % count) for i in range(ends)])]
    conv_general_dilated x5 -> x0, matrix products: 36 us -> none  [conv_local(): lax.conv_general_dilated(padded[None], kernel, (stride, stride), 'VALID',...]
    all_to_all x5 -> x0, starting transfers between devices: 35.3 us -> none  [from_everyone(): return lax.all_to_all(copies, axis, split_axis=0, concat_axis=0, tiled=True)]
    ppermute x20 -> x0, waiting for transfers between devices: 33.2 us -> none  [the longest x10 19.9 us: extended(): lax.ppermute(head, axis, [((i + 1) % count, i) for i in range(ends)])]
    another operation x5 -> x0, local copies, waits for them, and re-layouts: 21 us -> none  [conv_local(): kernel = kernel_rows.reshape(3, 3, width_in, kernel_rows.shape[1])]
    broadcast_in_dim x18 -> x0, local copies, waits for them, and re-layouts: 10.7 us -> none  [the longest x5 8.84 us: from_everyone(): copies = jnp.broadcast_to(value, (lax.axis_size(axis), *value.shape))]
  transfers between devices with their start and end apart: 25 -> 0, of which waited for: 11 -> 0; matrix products, arithmetic and copies ran while one was open for 25% -> 0% of each run, Pallas kernels for 0% -> 0%
where the time goes in v1:
time: 127 us; the launch traced here: 126 us
  Pallas kernels  122 us (96%)
  local copies, waits for them, and re-layouts  3.51 us (3%)
    pallas_call x1, Pallas kernels, local(): pl.pallas_call(kernel, out_shape=(jax.ShapeDtypeStruct((TH, TW, C), bf16)...  122 us
    unnamed x4, local copies, waits for them, and re-layouts  3.51 us

profile of v1, /device:TPU:1, one launch (start us, length us, event | category | flops | bytes accessed | tf_op | source)
XLA Modules:
  0.0 126.2 jit_solution(13383906745947921034)
XLA Ops:
  0.6 122.0 %down_block.1 = (bf16[32,64,320]{2,1,0:T(8,128)(2,1)}, bf16[16,32,320]{2,1,0:T(8,128)(2,1)}) custom-call(bf16[32,64,320]{2,1,0:T(8,128)(2,1)} %lat_hbm.1, bf16[5,180,320]{2,1,0:T(8,128)(2,1)} %w_hbm.1, f32[5,320]{1,0:T(8,128)} %bias_ref.1, f32[4,320]{1,0:T(4,128)} %gain_ref.1, f32[4,320]{1,0:T(4,128)} %shift_ref.1, f32[2,320]{1,0:T(2,128)} %time_ref.1), custom_call_target="tpu_custom_call" | custom-call | tf_op jit(solution)/shard_map/down_block/pallas_call | solution.py:451
  122.7 0.0 copy-start
  122.7 2.8 %copy.10 = bf16[32,64,320]{2,1,0:T(8,128)(2,1)} copy(bf16[32,64,320]{2,1,0:T(8,128)(2,1)} %get-tuple-element.4) | data formatting | bytes 2621440
  125.4 0.0 copy-done
  125.4 0.7 copy.11
Async XLA Ops:
  122.7 2.8 %copy-start = (bf16[16,32,320]{2,1,0:T(8,128)(2,1)S(1)}, bf16[16,32,320]{2,1,0:T(8,128)(2,1)}, u32[]{:S(2)}) copy-start(bf16[16,32,320]{2,1,0:T(8,128)(2,1)} %get-tuple-element.5) | copy-start | bytes 983044

commit v2 on v1

--- a/solution.py
+++ b/solution.py
@@ -1,4 +1,5 @@
 import functools
+import itertools
 
 import jax
 import jax.numpy as jnp
@@ -41,12 +42,21 @@
 WINDOWS = window_tiles()
 
 
+def others():
+    sizes = (NY, NX, NZ, NC)
+    steps = [o for o in itertools.product(*[range(n) for n in sizes]) if any(o)]
+    return sorted(steps, key=lambda o: -sum(2 * min(v, n - v) for v, n in zip(o[:3], sizes)) - o[3])
+
+
+OTHERS = others()
+
+
 def kernel(
     lat_hbm, w_hbm, bias_ref, gain_ref, shift_ref, time_ref,
     feat_hbm, red_hbm,
-    lat, wl, act_a, act_b, xs, r0, edge_mat, zs, ze, hc, es, cs, gath, wk, blockdiag,
-    ar_src, ar_a, ar_b, fbuf, rbuf,
-    sem_in, sem_out, ws_send, ws_recv, halo_send, halo_recv, ar_send, ar_recv,
+    lat, wl, act_a, act_b, xs, r0, edge_mat, zs, ze, hc, es, cs, gath, wk, to_group, to_channel,
+    ar_src, ar_got, fbuf, rbuf,
+    sem_in, sem_out, ws_send, ws_recv, halo_send, halo_recv, ar_send, ar_recv, everyone,
 ):
     y, x = lax.axis_index("rows_0"), lax.axis_index("rows_1")
     z, core = lax.axis_index("cols_0"), lax.axis_index("cols_1")
@@ -74,7 +84,6 @@
 
     barrier = pltpu.get_barrier_semaphore()
     peers = [row_peer(j) for j in range(1, NR)] + [col_peer(j) for j in range(1, NCOL)]
-    peers += [dev(up, left), dev(up, right), dev(down, left), dev(down, right)]
     for peer in peers:
         pl.semaphore_signal(barrier, inc=1, device_id=peer, device_id_type=MESH)
 
@@ -86,14 +95,25 @@
     row_id = lax.broadcasted_iota(jnp.int32, (96, SHARD), 0) + 96 * core
     col_id = lax.broadcasted_iota(jnp.int32, (96, SHARD), 1) + off
     place = jnp.where(row_id == col_id, 1.0, 0.0).astype(bf16)
-    for k in range(5):
+
+    def prepare(k):
         half = jnp.dot(place, wl[k], preferred_element_type=f32)
         gath[k, core, slot, 0:96] = half[:, 0:128].astype(bf16)
         gath[k, core, slot, 96:192] = half[:, 128:256].astype(bf16)
         tail = jnp.concatenate([half[0:48, 256:320], half[48:96, 256:320]], axis=1)
         gath[k, core, slot, 192:240] = tail.astype(bf16)
 
+    prepare(0)
+    ci = lax.broadcasted_iota(jnp.int32, (384, 128), 0)
+    gi = lax.broadcasted_iota(jnp.int32, (384, 128), 1)
+    to_group[...] = jnp.where(((ci * 6554) >> 16) == gi, 1.0, 0.0).astype(bf16)
+    ci = lax.broadcasted_iota(jnp.int32, (128, 384), 1)
+    gi = lax.broadcasted_iota(jnp.int32, (128, 384), 0)
+    to_channel[...] = jnp.where(((ci * 6554) >> 16) == gi, 1.0, 0.0).astype(bf16)
+
     pl.semaphore_wait(barrier, len(peers))
+    for j in range(1, NR):
+        pl.semaphore_signal(everyone, inc=1, device_id=row_peer(j), device_id_type=MESH)
 
     def along(step_minor, step_major):
         mi = lax.rem(minor + step_minor, 4)
@@ -160,13 +180,6 @@
                     tails.append(jnp.where(low, tile(t, 2), 0.0))
                 wbuf[row : row + 16, 768:896] = (tails[0] + pltpu.roll(tails[1], 64, 1)).astype(bf16)
                 wbuf[row : row + 16, 896:1024] = tails[2].astype(bf16)
-
-    for i in range(2):
-        wk[i, 960:1024, :] = jnp.zeros((64, 1024), bf16)
-    ci = lax.broadcasted_iota(jnp.int32, (384, 384), 0)
-    cj = lax.broadcasted_iota(jnp.int32, (384, 384), 1)
-    same = ((ci * 6554) >> 16) == ((cj * 6554) >> 16)
-    blockdiag[...] = jnp.where(same, 1.0, 0.0).astype(bf16)
 
     zero_acc = tuple(jnp.zeros((8, 128), f32) for _ in range(6))
 
@@ -202,44 +215,45 @@
             for i, (s, d, to) in enumerate(msgs)
         ]
 
-    def all_sum(phase, acc, between):
-        vec = jnp.concatenate(
-            [jnp.sum(v, axis=0, keepdims=True) for v in acc] + [jnp.zeros((2, 128), f32)], axis=0
+    def thirds(v):
+        hi = v.astype(bf16).astype(f32)
+        mid = (v - hi).astype(bf16).astype(f32)
+        return jnp.concatenate([hi, mid, v - hi - mid], axis=0).astype(bf16)
+
+    def send_sums(phase, acc):
+        sums = jnp.concatenate(
+            [jnp.concatenate(acc[0:3], axis=1), jnp.concatenate(acc[3:6], axis=1)], axis=0
         )
-        for stage, (buf, peer, n) in enumerate(((ar_a, col_peer, NCOL), (ar_b, row_peer, NR))):
-            src = ar_src.at[phase, stage]
-            src[...] = vec
-            for j in range(1, n):
-                pltpu.make_async_remote_copy(
-                    src, buf.at[phase, j - 1], ar_send.at[phase, stage], ar_recv.at[phase, stage], peer(j), MESH
-                ).start()
-            pending_sends.append((buf.at[phase], ar_send.at[phase, stage]))
-            between[stage]()
-            pltpu.make_async_copy(buf.at[phase], buf.at[phase], ar_recv.at[phase, stage]).wait()
-            vec = functools.reduce(lambda p, q: p + q, [vec] + [buf[phase, j] for j in range(n - 1)])
-        return vec
+        got = jnp.dot(thirds(sums), to_group[...], preferred_element_type=f32)
+        got = got[0:16] + got[16:32] + got[32:48]
+        own = jnp.sum(got[0:8], axis=0, keepdims=True) + pltpu.roll(jnp.sum(got[8:16], axis=0, keepdims=True), 32, 1)
+        ar_src[phase] = own
+        me = (y, x, z, core)
+        for j, offset in enumerate(OTHERS):
+            to = tuple(lax.rem(m + o, n) if o else m for m, o, n in zip(me, offset, (NY, NX, NZ, NC)))
+            pltpu.make_async_remote_copy(
+                ar_src.at[phase], ar_got.at[phase, j], ar_send.at[phase], ar_recv.at[phase], to, MESH
+            ).start()
+        pending_sends.append((ar_got.at[phase], ar_send.at[phase]))
+        return own
+
+    def all_sums(phase, own):
+        every = ar_got.at[phase]
+        pltpu.make_async_copy(every, every, ar_recv.at[phase]).wait()
+        return own + jnp.sum(ar_got[phase], axis=0)
 
     def scales(phase, vec):
-        both = jnp.concatenate(
-            [
-                jnp.concatenate([vec[0:1], vec[1:2], vec[2:3]], axis=1),
-                jnp.concatenate([vec[3:4], vec[4:5], vec[5:6]], axis=1),
-            ],
-            axis=0,
-        )
-        hi = both.astype(bf16).astype(f32)
-        mid = (both - hi).astype(bf16).astype(f32)
-        lo = both - hi - mid
-        parts = jnp.concatenate([hi, mid, lo, jnp.zeros((10, 384), f32)], axis=0).astype(bf16)
-        tot = jnp.dot(parts, blockdiag[...], preferred_element_type=f32)
-        sums = tot[0:1] + tot[2:3] + tot[4:5]
-        squares = tot[1:2] + tot[3:4] + tot[5:6]
         count = float(TH * NR * TW * NCOL * (C // 32))
-        mean = sums / count
-        spread = jnp.maximum(squares / count - mean * mean, 0.0)
-        scale = lax.rsqrt(spread + EPS) * padded(gain_ref[phase : phase + 1, :])
-        move = padded(shift_ref[phase : phase + 1, :]) - mean * scale
-        scale, move = 0.5 * scale, 0.5 * move
+        mean = vec / count
+        spread = jnp.maximum(pltpu.roll(mean, 96, 1) - mean * mean, 0.0)
+        scale = lax.rsqrt(spread + EPS)
+        pair = jnp.concatenate([scale, mean * scale], axis=0)
+        pair = jnp.where(lane < 32, pair, 0.0)
+        tot = jnp.dot(thirds(jnp.concatenate([pair, jnp.zeros((6, 128), f32)], axis=0)), to_channel[...], preferred_element_type=f32)
+        tot = tot[0:8] + tot[8:16] + tot[16:24]
+        gain = padded(0.5 * gain_ref[phase : phase + 1, :])
+        scale = tot[0:1] * gain
+        move = padded(0.5 * shift_ref[phase : phase + 1, :]) - tot[1:2] * gain
         return [scale[:, 128 * t : 128 * t + 128] for t in range(3)], [move[:, 128 * t : 128 * t + 128] for t in range(3)]
 
     def silu_of(v, scale, move):
@@ -268,7 +282,7 @@
     er = lax.broadcasted_iota(jnp.int32, (48, 1), 0)
     edge_rows = jnp.where(er < 8, top, jnp.where(er < 40, 1.0, bottom))
 
-    def normalize(phase, act, sc, mv):
+    def normalize(phase, act, sc, mv, between):
         def one(i, prev):
             m = jnp.where(i == 0, top, jnp.where(i == TH + 1, bottom, 1.0))
             tiles = []
@@ -279,7 +293,9 @@
             r0[i, :, :] = (prev + pltpu.roll(tiles[2], 64, 1)).astype(bf16)
             return tiles[2]
 
-        lax.fori_loop(0, TH + 2, one, jnp.zeros((TW, 128), f32))
+        prev = lax.fori_loop(0, TH // 2, one, jnp.zeros((TW, 128), f32))
+        between()
+        lax.fori_loop(TH // 2, TH + 2, one, prev)
         for side, mask in ((0, west), (1, east)):
             for t in range(3):
                 es[side, t] = silu_of(hc[phase, side, t], sc[t], mv[t]) * (edge_rows * mask)
@@ -364,40 +380,37 @@
         lat_copies[i].wait()
         acc = lax.fori_loop(8 * i, 8 * i + 8, read_latent, acc)
 
+    pl.semaphore_wait(everyone, NR - 1)
+
     def nothing():
         pass
 
     for k in range(4):
         act, res, out = (act_a, None, act_b) if k % 2 == 0 else (act_b, act_a, act_a)
+        own = send_sums(k, acc)
         halos = halo_messages(k, act)
         for h in halos:
             h.start()
         if k == 0:
-            def first_wait():
-                w_stage2(0)
-                w_stage1(1)
-
-            def second_wait():
-                w_swap(0)
-                w_stage2(1)
-                w_arrived(0)
-                relayout(0)
+            for later in range(1, 5):
+                prepare(later)
+            for i in range(2):
+                wk[i, 960:1024, :] = jnp.zeros((64, 1024), bf16)
+            w_stage2(0)
         else:
-            def first_wait(k=k):
-                w_arrived(k)
-                w_stage2(k + 1)
-
-            def second_wait(k=k):
-                relayout(k)
-        vec = all_sum(k, acc, (first_wait, second_wait))
-        sc, mv = scales(k, vec)
+            w_arrived(k)
+            relayout(k)
+        w_stage1(k + 1)
         for h in halos:
             h.wait()
+        sc, mv = scales(k, all_sums(k, own))
+        normalize(k, act, sc, mv, functools.partial(w_swap, 0) if k == 0 else nothing)
+        if k == 0:
+            w_arrived(0)
+            relayout(0)
+        w_stage2(k + 1)
+        acc = convolve(k, res, out)
         w_swap(k + 1)
-        if k < 3:
-            w_stage1(k + 2)
-        normalize(k, act, sc, mv)
-        acc = convolve(k, res, out)
 
     halos = halo_messages(4, act_a)
     for h in halos:
@@ -471,10 +484,10 @@
             pltpu.VMEM((5, 2, 3, TH, 128), f32),
             pltpu.VMEM((5, 2, NR, 240, 128), bf16),
             pltpu.VMEM((2, 1024, 1024), bf16),
-            pltpu.VMEM((384, 384), bf16),
-            pltpu.VMEM((4, 2, 8, 128), f32),
-            pltpu.VMEM((4, NCOL - 1, 8, 128), f32),
-            pltpu.VMEM((4, NR - 1, 8, 128), f32),
+            pltpu.VMEM((384, 128), bf16),
+            pltpu.VMEM((128, 384), bf16),
+            pltpu.VMEM((4, 1, 128), f32),
+            pltpu.VMEM((4, NR * NCOL - 1, 1, 128), f32),
             pltpu.VMEM((TH, TW, C), bf16),
             pltpu.VMEM((TH // 2, TW // 2, C), bf16),
             pltpu.SemaphoreType.DMA((5,)),
@@ -483,8 +496,9 @@
             pltpu.SemaphoreType.DMA((5, 3)),
             pltpu.SemaphoreType.DMA((5, 8)),
             pltpu.SemaphoreType.DMA((5, 8)),
-            pltpu.SemaphoreType.DMA((4, 2)),
-            pltpu.SemaphoreType.DMA((4, 2)),
+            pltpu.SemaphoreType.DMA((4,)),
+            pltpu.SemaphoreType.DMA((4,)),
+            pltpu.SemaphoreType.REGULAR,
         ],
         compiler_params=pltpu.CompilerParams(
             collective_id=0, has_side_effects=True, vmem_limit_bytes=60 * 1024 * 1024

time: 127 us -> 111 us (0.87)
  Pallas kernels: 122 us -> 107 us
    pallas_call x1, Pallas kernels: 122 us -> 107 us  [local(): pl.pallas_call(kernel, out_shape=(jax.ShapeDtypeStruct((TH, TW, C), bf16)...]
where the time goes in v2:
time: 111 us
  Pallas kernels  107 us (96%)
  local copies, waits for them, and re-layouts  3.51 us (3%)
    pallas_call x1, Pallas kernels, local(): pl.pallas_call(kernel, out_shape=(jax.ShapeDtypeStruct((TH, TW, C), bf16)...  107 us
    unnamed x4, local copies, waits for them, and re-layouts  3.51 us

profile of v2, /device:TPU:1, one launch (start us, length us, event | category | flops | bytes accessed | tf_op | source)
XLA Modules:
  0.0 111.2 jit_solution(10103352680681931998)
XLA Ops:
  0.6 107.0 %down_block.1 = (bf16[32,64,320]{2,1,0:T(8,128)(2,1)}, bf16[16,32,320]{2,1,0:T(8,128)(2,1)}) custom-call(bf16[32,64,320]{2,1,0:T(8,128)(2,1)} %lat_hbm.1, bf16[5,180,320]{2,1,0:T(8,128)(2,1)} %w_hbm.1, f32[5,320]{1,0:T(8,128)} %bias_ref.1, f32[4,320]{1,0:T(4,128)} %gain_ref.1, f32[4,320]{1,0:T(4,128)} %shift_ref.1, f32[2,320]{1,0:T(2,128)} %time_ref.1), custom_call_target="tpu_custom_call" | custom-call | tf_op jit(solution)/shard_map/down_block/pallas_call | solution.py:464
  107.6 0.0 copy-start
  107.7 2.8 %copy.10 = bf16[32,64,320]{2,1,0:T(8,128)(2,1)} copy(bf16[32,64,320]{2,1,0:T(8,128)(2,1)} %get-tuple-element.4) | data formatting | bytes 2621440
  110.4 0.0 copy-done
  110.4 0.7 copy.11
Async XLA Ops:
  107.6 2.8 %copy-start = (bf16[16,32,320]{2,1,0:T(8,128)(2,1)S(1)}, bf16[16,32,320]{2,1,0:T(8,128)(2,1)}, u32[]{:S(2)}) copy-start(bf16[16,32,320]{2,1,0:T(8,128)(2,1)} %get-tuple-element.5) | copy-start | bytes 983044

commit v3 on v2

--- a/solution.py
+++ b/solution.py
@@ -18,7 +18,8 @@
 C = 320
 TH, TW = 32, 64
 SHARD = 180
-RB = 16
+RB = 8
+NB = TH // RB
 EPS = 1e-05
 
 
@@ -54,9 +55,9 @@
 def kernel(
     lat_hbm, w_hbm, bias_ref, gain_ref, shift_ref, time_ref,
     feat_hbm, red_hbm,
-    lat, wl, act_a, act_b, xs, r0, edge_mat, zs, ze, hc, es, cs, gath, wk, to_group, to_channel,
-    ar_src, ar_got, fbuf, rbuf,
-    sem_in, sem_out, ws_send, ws_recv, halo_send, halo_recv, ar_send, ar_recv, everyone,
+    lat, wl, act_a, act_b, xs, r0, edge_mat, zs_even, zs_odd, hc, es, cs, gath, wk, to_group, to_channel,
+    ar_src, ar_got, ar_first, fbuf, rbuf,
+    sem_in, sem_out, ws_send, ws_recv, halo_send, halo_recv, ar_send, ar_recv,
 ):
     y, x = lax.axis_index("rows_0"), lax.axis_index("rows_1")
     z, core = lax.axis_index("cols_0"), lax.axis_index("cols_1")
@@ -112,8 +113,6 @@
     to_channel[...] = jnp.where(((ci * 6554) >> 16) == gi, 1.0, 0.0).astype(bf16)
 
     pl.semaphore_wait(barrier, len(peers))
-    for j in range(1, NR):
-        pl.semaphore_signal(everyone, inc=1, device_id=row_peer(j), device_id_type=MESH)
 
     def along(step_minor, step_major):
         mi = lax.rem(minor + step_minor, 4)
@@ -149,7 +148,6 @@
         every = gath.at[k, 0]
         pltpu.make_async_copy(every, every, ws_recv.at[k, 2]).wait()
 
-    w_stage1(0)
 
     lane = lax.broadcasted_iota(jnp.int32, (1, 128), 1)
     low = lane < 64
@@ -220,13 +218,15 @@
         mid = (v - hi).astype(bf16).astype(f32)
         return jnp.concatenate([hi, mid, v - hi - mid], axis=0).astype(bf16)
 
-    def send_sums(phase, acc):
+    def own_sums(acc):
         sums = jnp.concatenate(
             [jnp.concatenate(acc[0:3], axis=1), jnp.concatenate(acc[3:6], axis=1)], axis=0
         )
         got = jnp.dot(thirds(sums), to_group[...], preferred_element_type=f32)
         got = got[0:16] + got[16:32] + got[32:48]
-        own = jnp.sum(got[0:8], axis=0, keepdims=True) + pltpu.roll(jnp.sum(got[8:16], axis=0, keepdims=True), 32, 1)
+        return jnp.sum(got[0:8], axis=0, keepdims=True) + pltpu.roll(jnp.sum(got[8:16], axis=0, keepdims=True), 32, 1)
+
+    def send_sums(phase, own):
         ar_src[phase] = own
         me = (y, x, z, core)
         for j, offset in enumerate(OTHERS):
@@ -235,6 +235,21 @@
                 ar_src.at[phase], ar_got.at[phase, j], ar_send.at[phase], ar_recv.at[phase], to, MESH
             ).start()
         pending_sends.append((ar_got.at[phase], ar_send.at[phase]))
+
+    def first_sums(own, between):
+        at = 0
+        for stage, (peer, n) in enumerate(((col_peer, NCOL), (row_peer, NR))):
+            ar_src[4 + stage] = own
+            got = ar_first.at[pl.ds(at, n - 1)]
+            for j in range(1, n):
+                pltpu.make_async_remote_copy(
+                    ar_src.at[4 + stage], ar_first.at[at + j - 1], ar_send.at[4 + stage], ar_recv.at[4 + stage], peer(j), MESH
+                ).start()
+            pending_sends.append((got, ar_send.at[4 + stage]))
+            between[stage]()
+            pltpu.make_async_copy(got, got, ar_recv.at[4 + stage]).wait()
+            own = own + jnp.sum(ar_first[at : at + n - 1], axis=0)
+            at += n - 1
         return own
 
     def all_sums(phase, own):
@@ -266,55 +281,65 @@
     top, bottom = on(r > 0), on(r < NR - 1)
     west, east = on(c > 0), on(c < NCOL - 1)
 
-    def edges_to_matrix(rows, stride, sides):
-        for side in range(sides):
-            at = slice(rows * side, rows * side + rows)
-            taps = [
-                [es[side, t, pl.ds(7 + a, rows, stride=stride) if stride > 1 else pl.ds(7 + a, rows), :] for t in range(3)]
-                for a in range(3)
-            ]
-            for a in range(3):
-                for t in range(2):
-                    edge_mat[at, 256 * a + 128 * t : 256 * a + 128 * t + 128] = taps[a][t].astype(bf16)
-            edge_mat[at, 768:896] = (taps[0][2] + pltpu.roll(taps[1][2], 64, 1)).astype(bf16)
-            edge_mat[at, 896:1024] = taps[2][2].astype(bf16)
+    def edge_taps(side, rows, stride):
+        def tap(t, a):
+            if stride > 1:
+                return es[side, t, pl.ds(7 + a, rows, stride=stride), :]
+            return es[side, t, 7 + a : 7 + a + rows, :]
+
+        cols = [tap(t, a) for a in range(3) for t in range(2)]
+        return cols + [tap(2, 0) + pltpu.roll(tap(2, 1), 64, 1), tap(2, 2)]
+
+    def edges_to_matrix():
+        both = [edge_taps(side, TH, 1) for side in range(2)]
+        for b in range(NB):
+            for i in range(8):
+                pair = [both[side][i][RB * b : RB * b + RB] for side in range(2)]
+                edge_mat[2 * RB * b : 2 * RB * (b + 1), 128 * i : 128 * i + 128] = jnp.concatenate(pair, axis=0).astype(bf16)
 
     er = lax.broadcasted_iota(jnp.int32, (48, 1), 0)
     edge_rows = jnp.where(er < 8, top, jnp.where(er < 40, 1.0, bottom))
 
-    def normalize(phase, act, sc, mv, between):
-        def one(i, prev):
-            m = jnp.where(i == 0, top, jnp.where(i == TH + 1, bottom, 1.0))
+    def norm_rows(act, sc, mv, carry, rows):
+        for i in reversed(rows):
             tiles = []
             for t in range(3):
+                scale, move = sc[t], mv[t]
+                if i in (0, TH + 1):
+                    mask = top if i == 0 else bottom
+                    scale, move = scale * mask, move * mask
                 v = act[i, :, 128 * t : 128 * t + 128].astype(f32)
-                tiles.append(silu_of(v, sc[t] * m, mv[t] * m))
+                tiles.append(silu_of(v, scale, move))
                 xs[i, :, 128 * t : 128 * t + 128] = tiles[t].astype(bf16)
-            r0[i, :, :] = (prev + pltpu.roll(tiles[2], 64, 1)).astype(bf16)
-            return tiles[2]
-
-        prev = lax.fori_loop(0, TH // 2, one, jnp.zeros((TW, 128), f32))
-        between()
-        lax.fori_loop(TH // 2, TH + 2, one, prev)
+            if carry[0] is not None:
+                r0[i + 1] = (tiles[2] + carry[0]).astype(bf16)
+            carry[0] = pltpu.roll(tiles[2], 64, 1)
+
+    def norm_edges(phase, sc, mv):
         for side, mask in ((0, west), (1, east)):
             for t in range(3):
                 es[side, t] = silu_of(hc[phase, side, t], sc[t], mv[t]) * (edge_rows * mask)
-        edges_to_matrix(TH, 1, 2)
-
-    def edge_dot(k, rows):
-        for n in range(4):
-            o = jnp.dot(edge_mat[0:rows], wk[k % 2, :, 256 * n : 256 * n + 256], preferred_element_type=f32)
-            ze[2 * n, 0:rows] = o[:, 0:128]
-            ze[2 * n + 1, 0:rows] = o[:, 128:256]
-
-    def block_dot(k, parts):
-        lhs = jnp.concatenate(parts, axis=1)
+        edges_to_matrix()
+
+    def block_dot(k, zs, parts, edges, work):
+        lhs = jnp.concatenate([jnp.concatenate(parts, axis=1), edges], axis=0)
+        rows = RB * TW
         for n in range(4):
             o = jnp.dot(lhs, wk[k % 2, :, 256 * n : 256 * n + 256], preferred_element_type=f32)
-            zs[2 * n, :, 8 : 8 + TW, :] = o[:, 0:128].reshape(RB, TW, 128)
-            zs[2 * n + 1, :, 8 : 8 + TW, :] = o[:, 128:256].reshape(RB, TW, 128)
-
-    def taps_sum(rr, width, stride):
+            for t in range(2):
+                p = o[:, 128 * t : 128 * t + 128]
+                tile = 2 * n + t
+                zs[tile, :, 8 : 8 + TW, :] = p[0:rows].reshape(RB, TW, 128)
+                if tile in (0, 1, 6):
+                    for rr in range(RB):
+                        zs[tile, rr, 7:8, :] = p[rows + rr : rows + rr + 1]
+                if tile in (4, 5, 7):
+                    for rr in range(RB):
+                        zs[tile, rr, 8 + TW : 9 + TW, :] = p[rows + RB + rr : rows + RB + rr + 1]
+            for item in work[len(work) * n // 4 : len(work) * (n + 1) // 4]:
+                item()
+
+    def taps_sum(zs, rr, width, stride):
         def at(t, first):
             if stride > 1:
                 return zs[t, rr, pl.ds(first, width, stride=stride), :]
@@ -324,48 +349,62 @@
         tail = at(6, 7) + pltpu.roll(at(6, 8), 64, 1) + at(7, 9)
         return outs + [jnp.where(low, tail, 0.0)]
 
-    def place_edges(rr, row, rows, both):
-        for t in (0, 1, 6):
-            zs[t, rr, 7:8, :] = ze[t, pl.ds(row, 1), :]
-        if both:
-            for t in (4, 5, 7):
-                zs[t, rr, 72:73, :] = ze[t, pl.ds(rows + row, 1), :]
-
     def split(row):
         row = padded(row)
         return [row[:, 128 * t : 128 * t + 128] for t in range(3)]
 
-    def convolve(k, res, out):
+    def convolve(k, act, sc, mv, res, out, ahead):
         extra = split(bias_ref[k : k + 1, :] + (time_ref[k // 2 : k // 2 + 1, :] if k % 2 == 0 else 0.0))
-        edge_dot(k, 2 * TH)
-
-        def block(i, acc):
-            first = i * RB
-            parts = [xs[pl.ds(first + a, RB), :, 0:256].reshape(RB * TW, 256) for a in range(3)]
-            parts.append(r0[pl.ds(first + 1, RB)].reshape(RB * TW, 128))
-            parts.append(xs[pl.ds(first + 2, RB), :, 256:384].reshape(RB * TW, 128))
-            block_dot(k, parts)
-
-            def one(rr, acc):
-                row = first + rr
-                place_edges(rr, row, TH, True)
-                tiles = []
-                for t, o in enumerate(taps_sum(rr, TW, 1)):
-                    o = o + extra[t]
-                    if res is not None:
-                        o = o + res[row + 1, :, 128 * t : 128 * t + 128].astype(f32)
-                    o = o.astype(bf16)
-                    out[row + 1, :, 128 * t : 128 * t + 128] = o
-                    tiles.append(o.astype(f32))
-                stage_cols(k + 1, row, tiles)
-                if k == 3:
-                    fbuf[row] = jnp.concatenate([tiles[0], tiles[1], tiles[2][:, 0:64]], axis=1).astype(bf16)
-                    return acc
-                return add_stats(acc, tiles)
-
-            return lax.fori_loop(0, RB, one, acc)
-
-        return lax.fori_loop(0, TH // RB, block, zero_acc)
+        stats = [zero_acc]
+        carry = [None]
+
+        def norm_item(rows):
+            return lambda: norm_rows(act, sc, mv, carry, rows)
+
+        def needed(b):
+            return range(RB * b, RB * b + RB if b < NB - 1 else TH + 2)
+
+        def finish_row(zs, b, rr):
+            row = RB * b + rr
+            tiles = []
+            for t, o in enumerate(taps_sum(zs, rr, TW, 1)):
+                o = o + extra[t]
+                if res is not None:
+                    o = o + res[row + 1, :, 128 * t : 128 * t + 128].astype(f32)
+                o = o.astype(bf16)
+                out[row + 1, :, 128 * t : 128 * t + 128] = o
+                tiles.append(o.astype(f32))
+            for t in range(3):
+                cs[k + 1, 0, t, row : row + 1, :] = tiles[t][0:1]
+                cs[k + 1, 1, t, row : row + 1, :] = tiles[t][TW - 1 : TW]
+            if k == 3:
+                fbuf[row] = jnp.concatenate([tiles[0], tiles[1], tiles[2][:, 0:64]], axis=1).astype(bf16)
+            else:
+                stats[0] = add_stats(stats[0], tiles)
+
+        def finish_item(zs, b, rr):
+            return lambda: finish_row(zs, b, rr)
+
+        norm_rows(act, sc, mv, carry, needed(NB - 1))
+        if ahead is not None:
+            ahead[0]()
+            norm_rows(act, sc, mv, carry, range(0, RB * (NB - 1)))
+            ahead[1]()
+        before = []
+        for step, b in enumerate(reversed(range(NB))):
+            zs = zs_even if step % 2 == 0 else zs_odd
+            parts = [xs[RB * b + a : RB * b + a + RB, :, 0:256].reshape(RB * TW, 256) for a in range(3)]
+            parts.append(r0[RB * b + 1 : RB * b + 1 + RB].reshape(RB * TW, 128))
+            parts.append(xs[RB * b + 2 : RB * b + 2 + RB, :, 256:384].reshape(RB * TW, 128))
+            work = list(before)
+            if b > 0 and ahead is None:
+                norms = [norm_item(range(i, i + 1)) for i in reversed(needed(b - 1))]
+                work = [w for pair in itertools.zip_longest(norms, work) for w in pair if w is not None]
+            block_dot(k, zs, parts, edge_mat[2 * RB * b : 2 * RB * (b + 1)], work)
+            before = [finish_item(zs, b, rr) for rr in reversed(range(RB))]
+        for item in before:
+            item()
+        return stats[0]
 
     def read_latent(i, acc):
         v = lat[i].astype(f32)
@@ -380,36 +419,53 @@
         lat_copies[i].wait()
         acc = lax.fori_loop(8 * i, 8 * i + 8, read_latent, acc)
 
-    pl.semaphore_wait(everyone, NR - 1)
-
-    def nothing():
-        pass
+
+    w_stage1(0)
 
     for k in range(4):
         act, res, out = (act_a, None, act_b) if k % 2 == 0 else (act_b, act_a, act_a)
-        own = send_sums(k, acc)
+        own = own_sums(acc)
         halos = halo_messages(k, act)
-        for h in halos:
-            h.start()
+        straight = [h for i, h in enumerate(halos) if i in (0, 1, 3, 4)]
+        corners = [h for i, h in enumerate(halos) if i in (2, 5, 6, 7)]
+        ahead = None
         if k == 0:
-            for later in range(1, 5):
-                prepare(later)
-            for i in range(2):
-                wk[i, 960:1024, :] = jnp.zeros((64, 1024), bf16)
-            w_stage2(0)
+            def beside_first():
+                for h in straight:
+                    h.start()
+                for later in range(1, 5):
+                    prepare(later)
+                for i in range(2):
+                    wk[i, 960:1024, :] = jnp.zeros((64, 1024), bf16)
+
+            def beside_second():
+                for h in corners:
+                    h.start()
+                w_stage2(0)
+                w_stage1(1)
+
+            def got_first():
+                w_arrived(0)
+                w_stage2(1)
+                relayout(0)
+
+            ahead = (functools.partial(w_swap, 0), got_first)
+            total = first_sums(own, (beside_first, beside_second))
         else:
+            send_sums(k, own)
+            for h in straight + corners:
+                h.start()
             w_arrived(k)
             relayout(k)
-        w_stage1(k + 1)
+            w_stage1(k + 1)
+            total = all_sums(k, own)
+        sc, mv = scales(k, total)
         for h in halos:
             h.wait()
-        sc, mv = scales(k, all_sums(k, own))
-        normalize(k, act, sc, mv, functools.partial(w_swap, 0) if k == 0 else nothing)
-        if k == 0:
-            w_arrived(0)
-            relayout(0)
-        w_stage2(k + 1)
-        acc = convolve(k, res, out)
+        norm_edges(k, sc, mv)
+        if k > 0:
+            w_stage2(k + 1)
+        acc = convolve(k, act, sc, mv, res, out, ahead)
         w_swap(k + 1)
 
     halos = halo_messages(4, act_a)
@@ -419,38 +475,51 @@
     feat_copy.start()
     w_arrived(4)
     relayout(4)
+    half = TH // 2
+    extra4 = split(bias_ref[4:5, :])
+
+    def reduced_parts(b):
+        def every_other(first, lanes):
+            return jnp.concatenate([act_a[2 * p + first, :, lanes] for p in range(RB * b, RB * b + RB)], axis=0)
+
+        heads = [every_other(a, slice(0, 256)) for a in range(3)]
+        pair = every_other(0, slice(256, 384)).astype(f32) + pltpu.roll(every_other(1, slice(256, 384)).astype(f32), 64, 1)
+        return heads + [pair.astype(bf16), every_other(2, slice(256, 384))]
+
+    def dot4(zs, parts, edges):
+        lhs = jnp.concatenate(parts, axis=1)
+        rows = RB * TW
+        if edges is not None:
+            lhs = jnp.concatenate([lhs, edges], axis=0)
+        for n in range(4):
+            o = jnp.dot(lhs, wk[0, :, 256 * n : 256 * n + 256], preferred_element_type=f32)
+            for t in range(2):
+                tile = 2 * n + t
+                p = o[:, 128 * t : 128 * t + 128]
+                zs[tile, :, 8 : 8 + TW, :] = p[0:rows].reshape(RB, TW, 128)
+                if edges is not None and tile in (0, 1, 6):
+                    for rr in range(half):
+                        (zs_odd if rr < RB else zs_even)[tile, rr % RB, 7:8, :] = p[rows + rr : rows + rr + 1]
+
+    dot4(zs_even, reduced_parts(1), None)
     for h in halos:
         h.wait()
     for t in range(3):
         act_a[0, :, 128 * t : 128 * t + 128] = (act_a[0, :, 128 * t : 128 * t + 128].astype(f32) * top).astype(bf16)
         es[0, t] = hc[4, 0, t] * (edge_rows * west)
-    edges_to_matrix(TH // 2, 2, 1)
-
-    def tails4(p, carry):
-        pair = act_a[2 * p, :, 256:384].astype(f32) + pltpu.roll(act_a[2 * p + 1, :, 256:384].astype(f32), 64, 1)
-        r0[p, :, :] = pair.astype(bf16)
-        return carry
-
-    lax.fori_loop(0, TH // 2, tails4, 0)
-    edge_dot(4, TH // 2)
-    half = TH // 2
-
-    def every_other(first, lanes):
-        return jnp.concatenate([act_a[2 * p + first, :, lanes] for p in range(half)], axis=0)
-
-    parts = [every_other(a, slice(0, 256)) for a in range(3)]
-    parts.append(r0[0:half].reshape(half * TW, 128))
-    parts.append(every_other(2, slice(256, 384)))
-    block_dot(4, parts)
-    extra4 = split(bias_ref[4:5, :])
-
-    def last(p, carry):
-        place_edges(p, p, half, False)
-        tiles = [o + extra4[t] for t, o in enumerate(taps_sum(p, TW // 2, 2))]
-        rbuf[p] = jnp.concatenate([tiles[0], tiles[1], tiles[2][:, 0:64]], axis=1).astype(bf16)
-        return carry
-
-    lax.fori_loop(0, half, last, 0)
+    left_taps = jnp.concatenate(edge_taps(0, half, 2), axis=1).astype(bf16)
+    dot4(zs_odd, reduced_parts(0), left_taps)
+
+    def last(zs, first):
+        def one(p, carry):
+            tiles = [o + extra4[t] for t, o in enumerate(taps_sum(zs, p, TW // 2, 2))]
+            rbuf[first + p] = jnp.concatenate([tiles[0], tiles[1], tiles[2][:, 0:64]], axis=1).astype(bf16)
+            return carry
+
+        lax.fori_loop(0, RB, one, 0)
+
+    last(zs_even, RB)
+    last(zs_odd, 0)
     red_copy = pltpu.make_async_copy(rbuf, red_hbm, sem_out.at[1])
     red_copy.start()
     for ref, sem in pending_sends:
@@ -478,7 +547,7 @@
             pltpu.VMEM((TH + 2, TW, 128), bf16),
             pltpu.VMEM((2 * TH, 1024), bf16),
             pltpu.VMEM((8, RB, 80, 128), f32),
-            pltpu.VMEM((8, 2 * TH, 128), f32),
+            pltpu.VMEM((8, RB, 80, 128), f32),
             pltpu.VMEM((5, 2, 3, 48, 128), f32),
             pltpu.VMEM((2, 3, 48, 128), f32),
             pltpu.VMEM((5, 2, 3, TH, 128), f32),
@@ -486,8 +555,9 @@
             pltpu.VMEM((2, 1024, 1024), bf16),
             pltpu.VMEM((384, 128), bf16),
             pltpu.VMEM((128, 384), bf16),
-            pltpu.VMEM((4, 1, 128), f32),
+            pltpu.VMEM((6, 1, 128), f32),
             pltpu.VMEM((4, NR * NCOL - 1, 1, 128), f32),
+            pltpu.VMEM((NR + NCOL - 2, 1, 128), f32),
             pltpu.VMEM((TH, TW, C), bf16),
             pltpu.VMEM((TH // 2, TW // 2, C), bf16),
             pltpu.SemaphoreType.DMA((5,)),
@@ -496,9 +566,8 @@
             pltpu.SemaphoreType.DMA((5, 3)),
             pltpu.SemaphoreType.DMA((5, 8)),
             pltpu.SemaphoreType.DMA((5, 8)),
-            pltpu.SemaphoreType.DMA((4,)),
-            pltpu.SemaphoreType.DMA((4,)),
-            pltpu.SemaphoreType.REGULAR,
+            pltpu.SemaphoreType.DMA((6,)),
+            pltpu.SemaphoreType.DMA((6,)),
         ],
         compiler_params=pltpu.CompilerParams(
             collective_id=0, has_side_effects=True, vmem_limit_bytes=60 * 1024 * 1024

time: 111 us -> 94.4 us (0.85)
  Pallas kernels: 107 us -> 90 us
    pallas_call x1, Pallas kernels: 107 us -> 90 us  [local(): pl.pallas_call(kernel, out_shape=(jax.ShapeDtypeStruct((TH, TW, C), bf16)...]
where the time goes in v3:
time: 94.4 us; the launch traced here: 94.1 us
  Pallas kernels  90 us (95%)
  local copies, waits for them, and re-layouts  3.51 us (4%)
    pallas_call x1, Pallas kernels, local(): pl.pallas_call(kernel, out_shape=(jax.ShapeDtypeStruct((TH, TW, C), bf16)...  90 us
    unnamed x4, local copies, waits for them, and re-layouts  3.51 us

profile of v3, /device:TPU:1, one launch (start us, length us, event | category | flops | bytes accessed | tf_op | source)
XLA Modules:
  0.0 94.1 jit_solution(3634077171436039670)
XLA Ops:
  0.6 90.0 %down_block.1 = (bf16[32,64,320]{2,1,0:T(8,128)(2,1)}, bf16[16,32,320]{2,1,0:T(8,128)(2,1)}) custom-call(bf16[32,64,320]{2,1,0:T(8,128)(2,1)} %lat_hbm.1, bf16[5,180,320]{2,1,0:T(8,128)(2,1)} %w_hbm.1, f32[5,320]{1,0:T(8,128)} %bias_ref.1, f32[4,320]{1,0:T(4,128)} %gain_ref.1, f32[4,320]{1,0:T(4,128)} %shift_ref.1, f32[2,320]{1,0:T(2,128)} %time_ref.1), custom_call_target="tpu_custom_call" | custom-call | tf_op jit(solution)/shard_map/down_block/pallas_call | solution.py:533
  90.6 0.0 copy-start
  90.6 2.8 %copy.10 = bf16[32,64,320]{2,1,0:T(8,128)(2,1)} copy(bf16[32,64,320]{2,1,0:T(8,128)(2,1)} %get-tuple-element.4) | data formatting | bytes 2621440
  93.4 0.0 copy-done
  93.4 0.7 copy.11
Async XLA Ops:
  90.6 2.8 %copy-start = (bf16[16,32,320]{2,1,0:T(8,128)(2,1)S(1)}, bf16[16,32,320]{2,1,0:T(8,128)(2,1)}, u32[]{:S(2)}) copy-start(bf16[16,32,320]{2,1,0:T(8,128)(2,1)} %get-tuple-element.5) | copy-start | bytes 983044

commit v4 on v3

--- a/solution.py
+++ b/solution.py
@@ -112,7 +112,6 @@
     gi = lax.broadcasted_iota(jnp.int32, (128, 384), 0)
     to_channel[...] = jnp.where(((ci * 6554) >> 16) == gi, 1.0, 0.0).astype(bf16)
 
-    pl.semaphore_wait(barrier, len(peers))
 
     def along(step_minor, step_major):
         mi = lax.rem(minor + step_minor, 4)
@@ -353,7 +352,7 @@
         row = padded(row)
         return [row[:, 128 * t : 128 * t + 128] for t in range(3)]
 
-    def convolve(k, act, sc, mv, res, out, ahead):
+    def convolve(k, act, sc, mv, res, out, ahead, hooks):
         extra = split(bias_ref[k : k + 1, :] + (time_ref[k // 2 : k // 2 + 1, :] if k % 2 == 0 else 0.0))
         stats = [zero_acc]
         carry = [None]
@@ -393,6 +392,8 @@
         before = []
         for step, b in enumerate(reversed(range(NB))):
             zs = zs_even if step % 2 == 0 else zs_odd
+            if step in hooks:
+                hooks[step]()
             parts = [xs[RB * b + a : RB * b + a + RB, :, 0:256].reshape(RB * TW, 256) for a in range(3)]
             parts.append(r0[RB * b + 1 : RB * b + 1 + RB].reshape(RB * TW, 128))
             parts.append(xs[RB * b + 2 : RB * b + 2 + RB, :, 256:384].reshape(RB * TW, 128))
@@ -420,6 +421,7 @@
         acc = lax.fori_loop(8 * i, 8 * i + 8, read_latent, acc)
 
 
+    pl.semaphore_wait(barrier, len(peers))
     w_stage1(0)
 
     for k in range(4):
@@ -455,26 +457,40 @@
             send_sums(k, own)
             for h in straight + corners:
                 h.start()
+            w_swap(k)
+            if k == 3:
+                w_stage2(4)
+            else:
+                w_stage1(k + 1)
+                if k == 2:
+                    w_stage1(4)
             w_arrived(k)
             relayout(k)
-            w_stage1(k + 1)
             total = all_sums(k, own)
         sc, mv = scales(k, total)
         for h in halos:
             h.wait()
         norm_edges(k, sc, mv)
-        if k > 0:
+        hooks = {}
+        if k in (1, 2):
             w_stage2(k + 1)
-        acc = convolve(k, act, sc, mv, res, out, ahead)
-        w_swap(k + 1)
-
-    halos = halo_messages(4, act_a)
-    for h in halos:
-        h.start()
+        if k == 3:
+            last_halos = halo_messages(4, act_a)
+
+            def lowest_row_done():
+                last_halos[0].start()
+                last_halos[2].start()
+
+            def last_weights():
+                w_arrived(4)
+                relayout(4)
+
+            hooks = {1: functools.partial(w_swap, 4), 2: lowest_row_done, 3: last_weights}
+        acc = convolve(k, act, sc, mv, res, out, ahead, hooks)
+
+    last_halos[1].start()
     feat_copy = pltpu.make_async_copy(fbuf, feat_hbm, sem_out.at[0])
     feat_copy.start()
-    w_arrived(4)
-    relayout(4)
     half = TH // 2
     extra4 = split(bias_ref[4:5, :])
 
@@ -502,7 +518,7 @@
                         (zs_odd if rr < RB else zs_even)[tile, rr % RB, 7:8, :] = p[rows + rr : rows + rr + 1]
 
     dot4(zs_even, reduced_parts(1), None)
-    for h in halos:
+    for h in last_halos:
         h.wait()
     for t in range(3):
         act_a[0, :, 128 * t : 128 * t + 128] = (act_a[0, :, 128 * t : 128 * t + 128].astype(f32) * top).astype(bf16)

time: 94.4 us -> 85.2 us (0.903)
  Pallas kernels: 90 us -> 80.8 us
    pallas_call x1, Pallas kernels: 90 us -> 80.8 us  [local(): pl.pallas_call(kernel, out_shape=(jax.ShapeDtypeStruct((TH, TW, C), bf16)...]
where the time goes in v4:
time: 85.2 us; the launch traced here: 84.9 us
  Pallas kernels  80.8 us (95%)
  local copies, waits for them, and re-layouts  3.51 us (4%)
    pallas_call x1, Pallas kernels, local(): pl.pallas_call(kernel, out_shape=(jax.ShapeDtypeStruct((TH, TW, C), bf16)...  80.8 us
    unnamed x4, local copies, waits for them, and re-layouts  3.51 us

profile of v4, /device:TPU:1, one launch (start us, length us, event | category | flops | bytes accessed | tf_op | source)
XLA Modules:
  0.0 84.9 jit_solution(5488669887593416949)
XLA Ops:
  0.6 80.8 %down_block.1 = (bf16[32,64,320]{2,1,0:T(8,128)(2,1)}, bf16[16,32,320]{2,1,0:T(8,128)(2,1)}) custom-call(bf16[32,64,320]{2,1,0:T(8,128)(2,1)} %lat_hbm.1, bf16[5,180,320]{2,1,0:T(8,128)(2,1)} %w_hbm.1, f32[5,320]{1,0:T(8,128)} %bias_ref.1, f32[4,320]{1,0:T(4,128)} %gain_ref.1, f32[4,320]{1,0:T(4,128)} %shift_ref.1, f32[2,320]{1,0:T(2,128)} %time_ref.1), custom_call_target="tpu_custom_call" | custom-call | tf_op jit(solution)/shard_map/down_block/pallas_call | solution.py:549
  81.4 0.0 copy-start
  81.4 2.8 %copy.10 = bf16[32,64,320]{2,1,0:T(8,128)(2,1)} copy(bf16[32,64,320]{2,1,0:T(8,128)(2,1)} %get-tuple-element.4) | data formatting | bytes 2621440
  84.2 0.0 copy-done
  84.2 0.7 copy.11
Async XLA Ops:
  81.4 2.8 %copy-start = (bf16[16,32,320]{2,1,0:T(8,128)(2,1)S(1)}, bf16[16,32,320]{2,1,0:T(8,128)(2,1)}, u32[]{:S(2)}) copy-start(bf16[16,32,320]{2,1,0:T(8,128)(2,1)} %get-tuple-element.5) | copy-start | bytes 983044

commit v5 on v4

--- a/solution.py
+++ b/solution.py
@@ -544,14 +544,30 @@
     red_copy.wait()
 
 
+def hand_over(feat_from, red_from, feat_to, red_to, feat_buf, red_buf, sem_from, sem_to):
+    step = TH // 4
+    moves = [(feat_from.at[pl.ds(step * i, step)], feat_buf.at[pl.ds(step * i, step)], feat_to.at[pl.ds(step * i, step)]) for i in range(4)]
+    moves.append((red_from, red_buf, red_to))
+    reads = [pltpu.make_async_copy(a, b, sem_from.at[i]) for i, (a, b, _) in enumerate(moves)]
+    writes = [pltpu.make_async_copy(b, c, sem_to.at[i]) for i, (_, b, c) in enumerate(moves)]
+    for read in reads:
+        read.start()
+    for read, write in zip(reads, writes):
+        read.wait()
+        write.start()
+    for write in writes:
+        write.wait()
+
+
 def local(latent, conv_weights, conv_bias, norm_gain, norm_shift, time_shift):
     vmem, anywhere = pl.BlockSpec(memory_space=pltpu.VMEM), pl.BlockSpec(memory_space=pl.ANY)
-    return pl.pallas_call(
+    results = (
+        jax.ShapeDtypeStruct((TH, TW, C), bf16),
+        jax.ShapeDtypeStruct((TH // 2, TW // 2, C), bf16),
+    )
+    features, reduced = pl.pallas_call(
         kernel,
-        out_shape=(
-            jax.ShapeDtypeStruct((TH, TW, C), bf16),
-            jax.ShapeDtypeStruct((TH // 2, TW // 2, C), bf16),
-        ),
+        out_shape=results,
         in_specs=[anywhere, anywhere, vmem, vmem, vmem, vmem],
         out_specs=(anywhere, anywhere),
         scratch_shapes=[
@@ -590,6 +606,19 @@
         ),
         name="down_block",
     )(latent, conv_weights, conv_bias, norm_gain, norm_shift, time_shift)
+    return pl.pallas_call(
+        hand_over,
+        out_shape=results,
+        in_specs=[anywhere, anywhere],
+        out_specs=(anywhere, anywhere),
+        scratch_shapes=[
+            pltpu.VMEM((TH, TW, C), bf16),
+            pltpu.VMEM((TH // 2, TW // 2, C), bf16),
+            pltpu.SemaphoreType.DMA((5,)),
+            pltpu.SemaphoreType.DMA((5,)),
+        ],
+        name="hand_over",
+    )(features, reduced)
 
 
 def solution(mesh):

time: 85.2 us -> 84.2 us (0.988)
  local copies, waits for them, and re-layouts: 3.51 us -> 0 us
  Pallas kernels: 80.8 us -> 83.1 us
    unnamed x4 -> x0, local copies, waits for them, and re-layouts: 3.51 us -> none
    pallas_call x1 -> x2, Pallas kernels: 80.8 us -> 83.1 us  [the longest x1 80.8 us: local(): pl.pallas_call(kernel, out_shape=results, in_specs=[anywhere, anywhere, v...]
where the time goes in v5:
time: 84.2 us; the launch traced here: 83.9 us
  Pallas kernels  83.1 us (99%)
    pallas_call x1, Pallas kernels, local(): pl.pallas_call(kernel, out_shape=results, in_specs=[anywhere, anywhere, v...  80.8 us
    pallas_call x1, Pallas kernels, local(): pl.pallas_call(hand_over, out_shape=results, in_specs=[anywhere, anywhere...  2.35 us

profile of v5, /device:TPU:1, one launch (start us, length us, event | category | flops | bytes accessed | tf_op | source)
XLA Modules:
  0.0 83.9 jit_solution(8599259619630269101)
XLA Ops:
  0.6 80.8 %down_block.1 = (bf16[32,64,320]{2,1,0:T(8,128)(2,1)}, bf16[16,32,320]{2,1,0:T(8,128)(2,1)}) custom-call(bf16[32,64,320]{2,1,0:T(8,128)(2,1)} %lat_hbm.1, bf16[5,180,320]{2,1,0:T(8,128)(2,1)} %w_hbm.1, f32[5,320]{1,0:T(8,128)} %bias_ref.1, f32[4,320]{1,0:T(4,128)} %gain_ref.1, f32[4,320]{1,0:T(4,128)} %shift_ref.1, f32[2,320]{1,0:T(2,128)} %time_ref.1), custom_call_target="tpu_custom_call" | custom-call | tf_op jit(solution)/shard_map/down_block/pallas_call | solution.py:568
  81.4 2.3 %hand_over.1 = (bf16[32,64,320]{2,1,0:T(8,128)(2,1)}, bf16[16,32,320]{2,1,0:T(8,128)(2,1)}) custom-call(bf16[32,64,320]{2,1,0:T(8,128)(2,1)} %get-tuple-element.4.feat_from, bf16[16,32,320]{2,1,0:T(8,128)(2,1)} %get-tuple-element.5.red_from), custom_call_target="tpu_custom_call" | custom-call | tf_op jit(solution)/shard_map/hand_over/pallas_call | solution.py:609

commit v6 on v5

--- a/solution.py
+++ b/solution.py
@@ -387,7 +387,7 @@
         norm_rows(act, sc, mv, carry, needed(NB - 1))
         if ahead is not None:
             ahead[0]()
-            norm_rows(act, sc, mv, carry, range(0, RB * (NB - 1)))
+            norm_rows(act, sc, mv, carry, needed(NB - 2))
             ahead[1]()
         before = []
         for step, b in enumerate(reversed(range(NB))):
@@ -398,8 +398,9 @@
             parts.append(r0[RB * b + 1 : RB * b + 1 + RB].reshape(RB * TW, 128))
             parts.append(xs[RB * b + 2 : RB * b + 2 + RB, :, 256:384].reshape(RB * TW, 128))
             work = list(before)
-            if b > 0 and ahead is None:
-                norms = [norm_item(range(i, i + 1)) for i in reversed(needed(b - 1))]
+            later = b - 1 if ahead is None else b - 2
+            if later >= 0:
+                norms = [norm_item(range(i, i + 1)) for i in reversed(needed(later))]
                 work = [w for pair in itertools.zip_longest(norms, work) for w in pair if w is not None]
             block_dot(k, zs, parts, edge_mat[2 * RB * b : 2 * RB * (b + 1)], work)
             before = [finish_item(zs, b, rr) for rr in reversed(range(RB))]

time: 84.2 us -> 84.2 us (level)
  no operation moved by 1% of the time
where the time goes in v6:
time: 84.2 us; the launch traced here: 83.8 us
  Pallas kernels  83 us (99%)
    pallas_call x1, Pallas kernels, local(): pl.pallas_call(kernel, out_shape=results, in_specs=[anywhere, anywhere, v...  80.7 us
    pallas_call x1, Pallas kernels, local(): pl.pallas_call(hand_over, out_shape=results, in_specs=[anywhere, anywhere...  2.35 us

profile of v6, /device:TPU:1, one launch (start us, length us, event | category | flops | bytes accessed | tf_op | source)
XLA Modules:
  0.0 83.8 jit_solution(3634978724046374343)
XLA Ops:
  0.6 80.7 %down_block.1 = (bf16[32,64,320]{2,1,0:T(8,128)(2,1)}, bf16[16,32,320]{2,1,0:T(8,128)(2,1)}) custom-call(bf16[32,64,320]{2,1,0:T(8,128)(2,1)} %lat_hbm.1, bf16[5,180,320]{2,1,0:T(8,128)(2,1)} %w_hbm.1, f32[5,320]{1,0:T(8,128)} %bias_ref.1, f32[4,320]{1,0:T(4,128)} %gain_ref.1, f32[4,320]{1,0:T(4,128)} %shift_ref.1, f32[2,320]{1,0:T(2,128)} %time_ref.1), custom_call_target="tpu_custom_call" | custom-call | tf_op jit(solution)/shard_map/down_block/pallas_call | solution.py:569
  81.3 2.3 %hand_over.1 = (bf16[32,64,320]{2,1,0:T(8,128)(2,1)}, bf16[16,32,320]{2,1,0:T(8,128)(2,1)}) custom-call(bf16[32,64,320]{2,1,0:T(8,128)(2,1)} %get-tuple-element.4.feat_from, bf16[16,32,320]{2,1,0:T(8,128)(2,1)} %get-tuple-element.5.red_from), custom_call_target="tpu_custom_call" | custom-call | tf_op jit(solution)/shard_map/hand_over/pallas_call | solution.py:610

commit v7 on v6

--- a/solution.py
+++ b/solution.py
@@ -143,9 +143,31 @@
         ).start()
         pending_sends.append((gath.at[k, 0], ws_send.at[k, 2]))
 
+    def to_other_core(k, steps):
+        mine = gath.at[k, core, pl.ds(4 * lax.rem(major + steps, 4), 4)]
+        pltpu.make_async_remote_copy(
+            mine, mine, ws_send.at[k, 2], ws_recv.at[k, 4], (y, x, z, 1 - core), MESH
+        ).start()
+
+    def first_stage2(k):
+        three = gath.at[k, 0, 0:3]
+        pltpu.make_async_copy(three, three, ws_recv.at[k, 0]).wait()
+        mine = gath.at[k, core, pl.ds(4 * major, 4)]
+        for j in (2, 1, 3):
+            pltpu.make_async_remote_copy(mine, mine, ws_send.at[k, 1], ws_recv.at[k, j], along(0, j), MESH).start()
+        to_other_core(k, 0)
+        pending_sends.append((gath.at[k, 0, 0:12], ws_send.at[k, 1]))
+
+    def first_swap(k):
+        for j in (1, 3, 2):
+            four = gath.at[k, 0, 0:4]
+            pltpu.make_async_copy(four, four, ws_recv.at[k, j]).wait()
+            to_other_core(k, 4 - j)
+        pending_sends.append((gath.at[k, 0], ws_send.at[k, 2]))
+
     def w_arrived(k):
         every = gath.at[k, 0]
-        pltpu.make_async_copy(every, every, ws_recv.at[k, 2]).wait()
+        pltpu.make_async_copy(every, every, ws_recv.at[k, 4 if k == 0 else 2]).wait()
 
 
     lane = lax.broadcasted_iota(jnp.int32, (1, 128), 1)
@@ -444,7 +466,7 @@
             def beside_second():
                 for h in corners:
                     h.start()
-                w_stage2(0)
+                first_stage2(0)
                 w_stage1(1)
 
             def got_first():
@@ -452,7 +474,7 @@
                 w_stage2(1)
                 relayout(0)
 
-            ahead = (functools.partial(w_swap, 0), got_first)
+            ahead = (functools.partial(first_swap, 0), got_first)
             total = first_sums(own, (beside_first, beside_second))
         else:
             send_sums(k, own)
@@ -596,7 +618,7 @@
             pltpu.SemaphoreType.DMA((5,)),
             pltpu.SemaphoreType.DMA((2,)),
             pltpu.SemaphoreType.DMA((5, 3)),
-            pltpu.SemaphoreType.DMA((5, 3)),
+            pltpu.SemaphoreType.DMA((5, 5)),
             pltpu.SemaphoreType.DMA((5, 8)),
             pltpu.SemaphoreType.DMA((5, 8)),
             pltpu.SemaphoreType.DMA((6,)),

time: 84.2 us -> 84.4 us (level)
  no operation moved by 1% of the time
where the time goes in v7:
time: 84.4 us; the launch traced here: 83.9 us
  Pallas kernels  83.1 us (98%)
    pallas_call x1, Pallas kernels, local(): pl.pallas_call(kernel, out_shape=results, in_specs=[anywhere, anywhere, v...  80.8 us
    pallas_call x1, Pallas kernels, local(): pl.pallas_call(hand_over, out_shape=results, in_specs=[anywhere, anywhere...  2.35 us

profile of v7, /device:TPU:1, one launch (start us, length us, event | category | flops | bytes accessed | tf_op | source)
XLA Modules:
  0.0 83.9 jit_solution(8612219028879514168)
XLA Ops:
  0.6 80.8 %down_block.1 = (bf16[32,64,320]{2,1,0:T(8,128)(2,1)}, bf16[16,32,320]{2,1,0:T(8,128)(2,1)}) custom-call(bf16[32,64,320]{2,1,0:T(8,128)(2,1)} %lat_hbm.1, bf16[5,180,320]{2,1,0:T(8,128)(2,1)} %w_hbm.1, f32[5,320]{1,0:T(8,128)} %bias_ref.1, f32[4,320]{1,0:T(4,128)} %gain_ref.1, f32[4,320]{1,0:T(4,128)} %shift_ref.1, f32[2,320]{1,0:T(2,128)} %time_ref.1), custom_call_target="tpu_custom_call" | custom-call | tf_op jit(solution)/shard_map/down_block/pallas_call | solution.py:591
  81.4 2.3 %hand_over.1 = (bf16[32,64,320]{2,1,0:T(8,128)(2,1)}, bf16[16,32,320]{2,1,0:T(8,128)(2,1)}) custom-call(bf16[32,64,320]{2,1,0:T(8,128)(2,1)} %get-tuple-element.4.feat_from, bf16[16,32,320]{2,1,0:T(8,128)(2,1)} %get-tuple-element.5.red_from), custom_call_target="tpu_custom_call" | custom-call | tf_op jit(solution)/shard_map/hand_over/pallas_call | solution.py:632
